TPU v7x, 256 devices: a whole 4x4x8 slice. The times are simulated.
256 devices in a mesh: seq: 32 (over z_hi, x, core), head: 8 (over y, z_lo).
Axes of the slice: x: 4, y: 4, z: 8 (z_hi: 4, z_lo: 2; z = z_hi * 2 + z_lo), core: 2. Of those that a mesh axis runs over, the one named last changes fastest.
Arguments:
- queries: bfloat16 [512, 40, 128], P('seq', 'head'), may hold values from -6 to 6
- document_key_rows: bfloat16 [65536, 8, 128], P('seq', 'head'), may hold values from -16 to 16
- document_value_rows: bfloat16 [65536, 8, 128], P('seq', 'head'), may hold values from -6 to 6
- out_gain: float32 [40, 128], P('head'), may hold values from 0.1 to 1.9
- out_weight: bfloat16 [5120, 5120], P('head'), may hold values from -0.078125 to 0.078125
Outputs:
- mixed_out: bfloat16 [512, 5120], P('seq', 'head')
All inputs are finite; a program needn't handle non-finite values.
Results may differ from a plain program's by a relative error of at most 0.03.
Values may be sent and summed in bfloat16 or wider, within the bound.
No kernel may reach another device: no remote copies, remote signals or barrier semaphores. Data moves between devices by JAX's collectives and lax.ppermute only.
A program may use at most 64 MiB of HBM per device.

v0:
```python
import math

import jax
import jax.numpy as jnp
from jax import lax
from jax.sharding import PartitionSpec as P

SQRT_TWO = math.sqrt(2.0)


def feature_range(values_in, first_row, row_count):
    head_dim = values_in.shape[-1]
    last_axis = values_in.ndim - 1
    block_count = row_count // head_dim + 2
    first_shift = first_row // head_dim
    widened = values_in.astype(jnp.float32)
    doubled = jnp.concatenate([widened, widened], axis=last_axis)
    pieces = []
    for shift_index in range(block_count):
        shift_now = first_shift + shift_index
        shifted = lax.dynamic_slice_in_dim(doubled, shift_now, head_dim, last_axis)
        factor = jnp.where(shift_now == 0, 1.0, SQRT_TWO)
        pieces.append(widened * shifted * factor)
    joined = jnp.concatenate(pieces, axis=last_axis)
    chosen = lax.dynamic_slice_in_dim(
        joined, first_row - first_shift * head_dim, row_count, last_axis
    )
    return chosen.astype(jnp.bfloat16)


def block_width(row_count, unit_rows):
    multiple = row_count // unit_rows
    grouping = max([divisor for divisor in (1, 2, 4, 8) if multiple % divisor == 0])
    return unit_rows * grouping


def state_term(document_key_rows, document_value_rows, row_count, unit_rows):
    width_now = block_width(row_count, unit_rows)
    turns = row_count // width_now

    def one_block(turn_index):
        begin_row = turn_index * width_now
        key_feats = feature_range(document_key_rows, begin_row, width_now)
        return jnp.einsum(
            "tkf,tkd->fkd", key_feats, document_value_rows, preferred_element_type=jnp.float32
        )

    blocks = lax.map(one_block, jnp.arange(turns, dtype=jnp.int32))
    return blocks.reshape((row_count,) + blocks.shape[2:])


def on_device(queries, document_key_rows, document_value_rows, out_gain, out_weight):
    head_dim = document_key_rows.shape[-1]
    kv_local = document_key_rows.shape[1]
    query_local = queries.shape[1]
    query_group_width = query_local // kv_local
    feature_dim = head_dim * (head_dim + 1) // 2
    unit_rows = feature_dim // lax.axis_size("seq")
    own_first = lax.axis_index("seq") * unit_rows
    state_bf = lax.psum_scatter(
        state_term(
            document_key_rows, document_value_rows, unit_rows * lax.axis_size("seq"), unit_rows
        ).astype(jnp.bfloat16),
        "seq",
        scatter_dimension=0,
        tiled=True,
    )
    query_rows = lax.all_gather(queries, "seq", axis=0, tiled=True)
    query_feats = feature_range(
        query_rows.reshape(query_rows.shape[0], kv_local, query_group_width, head_dim),
        own_first,
        unit_rows,
    )
    read_out = jnp.einsum(
        "pkef,fkd->pked", query_feats, state_bf, preferred_element_type=jnp.float32
    )
    partial_rows = read_out.reshape(query_rows.shape[0], query_local, head_dim)
    retained = lax.psum_scatter(
        partial_rows.astype(jnp.bfloat16), "seq", scatter_dimension=0, tiled=True
    ).astype(jnp.float32)
    mean_square = jnp.mean(retained * retained, axis=-1, keepdims=True)
    normed = (retained * lax.rsqrt(mean_square + 1e-06) * out_gain).astype(jnp.bfloat16)
    flat = normed.reshape(normed.shape[0], query_local * head_dim)
    projected = jnp.dot(flat, out_weight, preferred_element_type=jnp.float32)
    return lax.psum_scatter(projected.astype(jnp.bfloat16), "head", scatter_dimension=1, tiled=True)


def solution(mesh):
    in_specs = (
        P("seq", "head", None),
        P("seq", "head", None),
        P("seq", "head", None),
        P("head", None),
        P("head", None),
    )
    out_specs = P("seq", "head")
    return jax.shard_map(
        on_device, mesh=mesh, in_specs=in_specs, out_specs=out_specs, check_vma=False
    )
```

profile of v0, /device:TPU:32, one launch (start us, length us, event | category | flops | bytes accessed | tf_op | source)
XLA Modules:
  0.0 455.4 jit_solution(3447157495574071604)
XLA Ops:
  6.5 156.3 %while.12 = (s32[]{:T(128)}, bf16[4,2064,1,128]{3,1,2,0:T(8,128)(2,1)}, bf16[2048,1,128]{2,0,1:T(8,128)(2,1)}, s32[4]{0:T(128)S(1)}, bf16[2048,1,128]{2,0,1:T(8,...) while((s32[]{:T(128)}, ...), condition=%wide.region_1.2_spmd, body=%wide.region_0.1_spmd.sunk | while | flops 1101267072 | bytes 63449552 | solution.py:48
  8.8 2.5 fusion.124
  20.1 1.5 fusion.131
  33.3 1.5 fusion.140
  36.3 9.4 %fusion.142 = bf16[4,2064,1,128]{3,1,2,0:T(8,128)(2,1)} fusion(bf16[4,2064,1,128]{3,1,2,0:T(8,128)(2,1)} %get-tuple-element.183, s32[]{:T(128)} %get-tuple-element.182, bf16[2048,1,2304]{2,0,1:T(8,128)(2,1)} %fusion.141, s32[]{:T(128)S(6)} %select_n.346, bf16[2048,1,128]{2,0,1:T(8,128)(2,1)S(1)} %copy-done.4), kind=kOutput, calls=%fused_computation.58.clone.1 | convolution fusion | flops 1082130432 | bytes 10494468 | tf_op jit(solution)/shard_map/while/body/eval_jaxpr/tkf,tkd->fkd/dot_general | solution.py:44
  47.9 2.5 fusion.124
  59.1 1.5 fusion.131
  72.3 1.5 fusion.140
  75.3 9.4 %fusion.142 = bf16[4,2064,1,128]{3,1,2,0:T(8,128)(2,1)} fusion(bf16[4,2064,1,128]{3,1,2,0:T(8,128)(2,1)} %get-tuple-element.183, s32[]{:T(128)} %get-tuple-element.182, bf16[2048,1,2304]{2,0,1:T(8,128)(2,1)} %fusion.141, s32[]{:T(128)S(6)} %select_n.346, bf16[2048,1,128]{2,0,1:T(8,128)(2,1)S(1)} %copy-done.4), kind=kOutput, calls=%fused_computation.58.clone.1 | convolution fusion | flops 1082130432 | bytes 10494468 | tf_op jit(solution)/shard_map/while/body/eval_jaxpr/tkf,tkd->fkd/dot_general | solution.py:44
  86.9 2.5 fusion.124
  98.2 1.5 fusion.131
  111.4 1.5 fusion.140
  114.4 9.4 %fusion.142 = bf16[4,2064,1,128]{3,1,2,0:T(8,128)(2,1)} fusion(bf16[4,2064,1,128]{3,1,2,0:T(8,128)(2,1)} %get-tuple-element.183, s32[]{:T(128)} %get-tuple-element.182, bf16[2048,1,2304]{2,0,1:T(8,128)(2,1)} %fusion.141, s32[]{:T(128)S(6)} %select_n.346, bf16[2048,1,128]{2,0,1:T(8,128)(2,1)S(1)} %copy-done.4), kind=kOutput, calls=%fused_computation.58.clone.1 | convolution fusion | flops 1082130432 | bytes 10494468 | tf_op jit(solution)/shard_map/while/body/eval_jaxpr/tkf,tkd->fkd/dot_general | solution.py:44
  126.0 2.5 fusion.124
  150.5 1.5 fusion.140
  153.5 9.4 %fusion.142 = bf16[4,2064,1,128]{3,1,2,0:T(8,128)(2,1)} fusion(bf16[4,2064,1,128]{3,1,2,0:T(8,128)(2,1)} %get-tuple-element.183, s32[]{:T(128)} %get-tuple-element.182, bf16[2048,1,2304]{2,0,1:T(8,128)(2,1)} %fusion.141, s32[]{:T(128)S(6)} %select_n.346, bf16[2048,1,128]{2,0,1:T(8,128)(2,1)S(1)} %copy-done.4), kind=kOutput, calls=%fused_computation.58.clone.1 | convolution fusion | flops 1082130432 | bytes 10494468 | tf_op jit(solution)/shard_map/while/body/eval_jaxpr/tkf,tkd->fkd/dot_general | solution.py:44
  162.9 91.6 %fusion = bf16[272,128]{1,0:T(8,128)(2,1)S(1)} fusion(bf16[8256,1,128]{2,0,1:T(8,128)(2,1)} %bitcast.67), kind=kCustom, calls=%all-reduce-scatter | all-reduce-scatter fusion | flops 1114113 | bytes 2184192
  257.2 40.9 %all_gather.3 = bf16[512,5,128]{2,0,1:T(8,128)(2,1)S(1)} all-gather(bf16[16,5,128]{2,0,1:T(8,128)(2,1)S(1)} %copy-done.1), channel_id=1, replica_groups=mesh['seq'=32,'head'=8] {'seq'}, dimensions={0}, use_global_device_ids=true | all-gather | bytes 675840 | tf_op jit(solution)/shard_map/all_gather | solution.py:68
  298.5 2.8 fusion.81
  303.4 2.1 fusion.88
  306.9 91.2 %reduce-scatter.8.cloned.1.call-done = bf16[16,5,128]{2,1,0:T(8,128)(2,1)} async-done(((bf16[512,5,128]{2,1,0:T(8,128)(2,1)}), bf16[16,5,128]{2,1,0:T(8,128)(2,1)}) %reduce-scatter.8.cloned.1.call-update) | async-done | bytes 20496 | tf_op jit(solution)/shard_map/reduce_scatter | solution.py:78
  399.9 3.8 convolution_convert_fusion
  405.2 41.8 %reduce-scatter.10.cloned.1.call-done = bf16[640,16]{1,0:T(8,128)(2,1)} async-done(((bf16[5120,16]{1,0:T(8,128)(2,1)}), bf16[640,16]{1,0:T(8,128)(2,1)}) %reduce-scatter.10.cloned.1.call-update) | async-done | bytes 20496
  447.0 1.6 copy.14
  (111 shorter events, 105.0 us)
Async XLA Ops:
  6.5 391.6 %reduce-scatter.8.cloned.1.call-start = ((), (), s32[]{:S(2)}) async-start(), calls=%async_computation.2 | async-start | bytes 1081344 | tf_op jit(solution)/shard_map/reduce_scatter | solution.py:78
  6.5 4.8 %copy-start = (bf16[2048,1,128]{2,0,1:T(8,128)(2,1)S(1)}, bf16[2048,1,128]{2,0,1:T(8,128)(2,1)}, u32[]{:S(2)}) copy-start(bf16[2048,1,128]{2,0,1:T(8,128)(2,1)} %get-tuple-element.232) | copy-start | bytes 1572868 | tf_op jit(solution)/shard_map/while
  33.3 3.0 copy-start.4
  45.6 4.8 %copy-start = (bf16[2048,1,128]{2,0,1:T(8,128)(2,1)S(1)}, bf16[2048,1,128]{2,0,1:T(8,128)(2,1)}, u32[]{:S(2)}) copy-start(bf16[2048,1,128]{2,0,1:T(8,128)(2,1)} %get-tuple-element.232) | copy-start | bytes 1572868 | tf_op jit(solution)/shard_map/while
  72.3 3.0 copy-start.4
  84.7 4.8 %copy-start = (bf16[2048,1,128]{2,0,1:T(8,128)(2,1)S(1)}, bf16[2048,1,128]{2,0,1:T(8,128)(2,1)}, u32[]{:S(2)}) copy-start(bf16[2048,1,128]{2,0,1:T(8,128)(2,1)} %get-tuple-element.232) | copy-start | bytes 1572868 | tf_op jit(solution)/shard_map/while
  111.4 3.0 copy-start.4
  123.8 4.8 %copy-start = (bf16[2048,1,128]{2,0,1:T(8,128)(2,1)S(1)}, bf16[2048,1,128]{2,0,1:T(8,128)(2,1)}, u32[]{:S(2)}) copy-start(bf16[2048,1,128]{2,0,1:T(8,128)(2,1)} %get-tuple-element.232) | copy-start | bytes 1572868 | tf_op jit(solution)/shard_map/while
  150.5 3.0 copy-start.4
  162.9 94.3 %copy-start.1 = (bf16[16,5,128]{2,0,1:T(8,128)(2,1)S(1)}, bf16[16,5,128]{2,0,1:T(8,128)(2,1)}, u32[]{:S(2)}) copy-start(bf16[16,5,128]{2,0,1:T(8,128)(2,1)} %param.7) | copy-start | bytes 61444
  254.5 48.1 %collective-permute-start = (bf16[272,128]{1,0:T(8,128)(2,1)S(1)}, bf16[272,128]{1,0:T(8,128)(2,1)S(1)}, u32[]{:S(2)}, u32[]{:S(2)}) collective-permute-start(bf16[272,128]{1,0:T(8,128)(2,1)S(1)} %fusion), channel_id=1, source_target_pairs={{0,8},{8,16},{16,24},{24,32},{32,40},{40,48},{48,56},{56,64},{64,7... | collective-permute-start | bytes 208904
  255.8 46.7 %collective-permute-start.1 = (bf16[162,128]{1,0:T(8,128)(2,1)S(1)}, bf16[162,128]{1,0:T(8,128)(2,1)S(1)}, u32[]{:S(2)}, u32[]{:S(2)}) collective-permute-start(bf16[162,128]{1,0:T(8,128)(2,1)S(1)} %slice), channel_id=1, source_target_pairs={{0,16},{8,24},{16,32},{24,40},{32,48},{40,56},{48,64},{56,72},{64,... | collective-permute-start | bytes 124424
  298.5 2.8 copy-start.3
  305.4 93.6 %copy-start.2 = (f32[5,128]{1,0:T(8,128)S(1)}, f32[5,128]{1,0:T(8,128)}, u32[]{:S(2)}) copy-start(f32[5,128]{1,0:T(8,128)} %param.10) | copy-start | bytes 7684
  306.9 140.1 %reduce-scatter.10.cloned.1.call-start = ((), (), s32[]{:S(2)}) async-start(), calls=%async_computation.3 | async-start | bytes 1474560
Sparse Core Ops, SparseCore 0:
  307.0 91.1 reduce-scatter.7
  405.3 41.5 reduce-scatter.9
where the time goes:
time: 459 us; the launch traced here: 455 us
  waiting for transfers between devices  133 us (29%)
  blocking collectives  132 us (29%)
  other arithmetic  119 us (26%)
  matrix products  43.3 us (9%)
  between operations  14.3 us (3%)
  local copies, waits for them, and re-layouts  8.44 us (2%)
    while x68, other arithmetic  104 us
    unnamed x1, blocking collectives  91.6 us
    reduce_scatter x1, waiting for transfers between devices, on_device(): lax.psum_scatter(partial_rows.astype(jnp.bfloat16), 'seq', scatter_dimens...  91.2 us
    unnamed x5, waiting for transfers between devices  41.8 us
    all_gather x1, blocking collectives, on_device(): query_rows = lax.all_gather(queries, 'seq', axis=0, tiled=True)  40.9 us
    dot_general x4, matrix products, one_block(): jnp.einsum('tkf,tkd->fkd', key_feats, document_value_rows, preferred_elem...  37.5 us
  transfers between devices with their start and end apart: 4, of which 2 were waited for; matrix products, arithmetic and copies ran while one was open for 1% of the time, Pallas kernels for 0%

commit v1 on v0

v1 whole, which is shorter than its diff:
```python
import jax
import jax.numpy as jnp
from jax import lax
from jax.experimental import pallas as pl
from jax.experimental.pallas import tpu as pltpu
from jax.sharding import PartitionSpec as P

CONTRACT_LAST = (((1,), (1,)), ((), ()))
KEY_TILE = 256
X_CHIPS, Z_BLOCKS, CORES = 4, 4, 2


def seq_index(z_block, x_chip, core):
    return (z_block * X_CHIPS + x_chip) * CORES + core


def same_core_groups():
    return [
        [seq_index(z, x, core) for z in range(Z_BLOCKS) for x in range(X_CHIPS)]
        for core in range(CORES)
    ]


def read_kernel(q_ref, k0_ref, k1_ref, v0_ref, v1_ref, o_ref):
    rows = q_ref[...]
    total = None
    for k_ref, v_ref in ((k0_ref, v0_ref), (k1_ref, v1_ref)):
        for start in range(0, k_ref.shape[0], KEY_TILE):
            tile = pl.ds(start, KEY_TILE)
            scores = lax.dot_general(
                rows, k_ref[tile, :], CONTRACT_LAST, preferred_element_type=jnp.float32
            )
            weights = (scores * scores).astype(jnp.bfloat16)
            term = jnp.dot(weights, v_ref[tile, :], preferred_element_type=jnp.float32)
            total = term if total is None else total + term
    o_ref[...] = total.astype(o_ref.dtype)


def read_document(rows, keys, values):
    vmem = pl.BlockSpec(memory_space=pltpu.VMEM)
    return pl.pallas_call(
        read_kernel,
        out_shape=jax.ShapeDtypeStruct(rows.shape, jnp.bfloat16),
        in_specs=[vmem] * 5,
        out_specs=vmem,
        compiler_params=pltpu.CompilerParams(vmem_limit_bytes=24 << 20),
        name="read_document",
    )(rows, *keys, *values)


def project_kernel(parts_ref, gain_ref, weight_ref, o_ref):
    retained = jnp.sum(parts_ref[...].astype(jnp.float32), axis=0)
    heads, width = gain_ref.shape
    rows = retained.shape[0] // heads
    pieces = []
    for h in range(heads):
        one = retained[h * rows : (h + 1) * rows, :]
        mean_square = jnp.mean(one * one, axis=-1, keepdims=True)
        normed = one * lax.rsqrt(mean_square + 1e-06) * gain_ref[pl.ds(h, 1), :]
        pieces.append(normed.astype(jnp.bfloat16))
    flat = jnp.concatenate(pieces, axis=1)
    chunk = o_ref.shape[2]
    for g in range(o_ref.shape[0]):
        o_ref[g] = jnp.dot(
            flat, weight_ref[:, g * chunk : (g + 1) * chunk], preferred_element_type=jnp.float32
        ).astype(o_ref.dtype)


def project(parts, gain, weight, groups):
    vmem = pl.BlockSpec(memory_space=pltpu.VMEM)
    rows = parts.shape[1] // gain.shape[0]
    return pl.pallas_call(
        project_kernel,
        out_shape=jax.ShapeDtypeStruct((groups, rows, weight.shape[1] // groups), jnp.bfloat16),
        in_specs=[vmem] * 3,
        out_specs=vmem,
        compiler_params=pltpu.CompilerParams(vmem_limit_bytes=24 << 20),
        name="project",
    )(parts, gain, weight)


def on_device(queries, document_key_rows, document_value_rows, out_gain, out_weight):
    rows, heads, width = queries.shape
    tokens = document_key_rows.shape[0]
    peers = same_core_groups()
    peer_count = len(peers[0])
    head_groups = lax.axis_size("head")
    keys = document_key_rows.reshape(tokens, width)
    values = document_value_rows.reshape(tokens, width)
    other_core = [(i, i ^ 1) for i in range(lax.axis_size("seq"))]
    other_keys = lax.ppermute(keys, "seq", other_core)
    other_values = lax.ppermute(values, "seq", other_core)
    own = jnp.transpose(queries, (1, 0, 2)).reshape(heads * rows, width)
    copies = jnp.broadcast_to(own[None], (peer_count, heads * rows, width))
    gathered = lax.all_to_all(copies, "seq", 0, 0, axis_index_groups=peers, tiled=True)
    partial = read_document(
        gathered.reshape(peer_count * heads * rows, width),
        (keys, other_keys),
        (values, other_values),
    ).reshape(peer_count, heads * rows, width)
    parts = lax.all_to_all(partial, "seq", 0, 0, axis_index_groups=peers, tiled=True)
    projected = project(parts, out_gain, out_weight, head_groups)
    pieces = lax.all_to_all(projected, "head", 0, 0, tiled=True)
    return jnp.sum(pieces.astype(jnp.float32), axis=0).astype(jnp.bfloat16)


def solution(mesh):
    in_specs = (
        P("seq", "head", None),
        P("seq", "head", None),
        P("seq", "head", None),
        P("head", None),
        P("head", None),
    )
    out_specs = P("seq", "head")
    return jax.shard_map(
        on_device, mesh=mesh, in_specs=in_specs, out_specs=out_specs, check_vma=False
    )
```

time: 459 us -> 67.7 us (0.15)
  waiting for transfers between devices: 133 us -> 13.3 us
  other arithmetic: 119 us -> 0.63 us
  blocking collectives: 132 us -> 28.3 us
  matrix products: 43.3 us -> 0 us
  between operations: 14.3 us -> 0.03 us
  starting transfers between devices: 2.63 us -> 10.7 us
  Pallas kernels: 0 us -> 7.11 us
    while x68 -> x0, other arithmetic: 104 us -> none
    unnamed x1 -> x0, blocking collectives: 91.6 us -> none
    reduce_scatter x1 -> x0, waiting for transfers between devices: 91.2 us -> none  [on_device(): lax.psum_scatter(partial_rows.astype(jnp.bfloat16), 'seq', scatter_dimens...]
    dot_general x6 -> x0, matrix products: 43.3 us -> none  [the longest x4 37.5 us: one_block(): jnp.einsum('tkf,tkd->fkd', key_feats, document_value_rows, preferred_elem...]
    unnamed x5 -> x0, waiting for transfers between devices: 41.8 us -> none
    all_gather x1 -> x0, blocking collectives: 40.9 us -> none  [on_device(): query_rows = lax.all_gather(queries, 'seq', axis=0, tiled=True)]
    all_to_all x0 -> x2, blocking collectives: none -> 28.3 us  [the longest x1 17 us: on_device(): lax.all_to_all(partial, 'seq', 0, 0, axis_index_groups=peers, tiled=True)]
    all_to_all x0 -> x1, waiting for transfers between devices: none -> 10.9 us  [on_device(): lax.all_to_all(copies, 'seq', 0, 0, axis_index_groups=peers, tiled=True)]
  transfers between devices with their start and end apart: 4 -> 3, of which waited for: 2 -> 3; matrix products, arithmetic and copies ran while one was open for 1% -> 0% of each run, Pallas kernels for 0% -> 0%
where the time goes in v1:
time: 67.7 us; the launch traced here: 67.3 us
  blocking collectives  28.3 us (42%)
  waiting for transfers between devices  13.3 us (20%)
  starting transfers between devices  10.7 us (16%)
  local copies, waits for them, and re-layouts  7.12 us (11%)
  Pallas kernels  7.11 us (11%)
    all_to_all x1, blocking collectives, on_device(): lax.all_to_all(partial, 'seq', 0, 0, axis_index_groups=peers, tiled=True)  17 us
    all_to_all x1, blocking collectives, on_device(): pieces = lax.all_to_all(projected, 'head', 0, 0, tiled=True)  11.3 us
    all_to_all x1, waiting for transfers between devices, on_device(): lax.all_to_all(copies, 'seq', 0, 0, axis_index_groups=peers, tiled=True)  10.9 us
    all_to_all x1, starting transfers between devices, on_device(): lax.all_to_all(copies, 'seq', 0, 0, axis_index_groups=peers, tiled=True)  10.1 us
    pallas_call x1, Pallas kernels, read_document(): pl.pallas_call(read_kernel, out_shape=jax.ShapeDtypeStruct(rows.shape, jn...  6.04 us
    unnamed x8, local copies, waits for them, and re-layouts  5.63 us
    ppermute x1, waiting for transfers between devices, on_device(): other_keys = lax.ppermute(keys, 'seq', other_core)  1.61 us
    broadcast_in_dim x1, local copies, waits for them, and re-layouts, on_device(): copies = jnp.broadcast_to(own[None], (peer_count, heads * rows, width))  1.49 us
  transfers between devices with their start and end apart: 3, of which 3 were waited for; matrix products, arithmetic and copies ran while one was open for 0% of the time, Pallas kernels for 0%

profile of v1, /device:TPU:32, one launch (start us, length us, event | category | flops | bytes accessed | tf_op | source)
XLA Modules:
  0.0 67.3 jit_solution(15203754206938529151)
XLA Ops:
  0.0 1.5 %broadcast_in_dim.8 = bf16[16,80,128]{2,1,0:T(8,128)(2,1)} broadcast(bf16[80,128]{1,0:T(8,128)(2,1)} %bitcast.13), dimensions={1,2} | broadcast | bytes 348160 | tf_op jit(solution)/shard_map/broadcast_in_dim | solution.py:94
  1.5 10.1 %all-to-all-start = ((bf16[16,80,128]{2,1,0:T(8,128)(2,1)}), bf16[16,80,128]{2,1,0:T(8,128)(2,1)S(1)}, u32[]{:S(2)}, u32[]{:S(2)}) async-start(bf16[16,80,128]{2,1,0:T(8,128)(2,1)} %broadcast_in_dim.8), calls=%async_computation | async-start | bytes 655360 | tf_op jit(solution)/shard_map/all_to_all | solution.py:95
  11.6 0.1 collective-permute-start
  11.7 0.5 collective-permute-start.1
  12.2 1.6 %collective-permute-done.k1_ref = bf16[2048,128]{1,0:T(8,128)(2,1)S(1)} collective-permute-done((bf16[2048,128]{1,0:T(8,128)(2,1)}, bf16[2048,128]{1,0:T(8,128)(2,1)S(1)}, u32[]{:S(2)}, u32[]{:S(2)}) %collective-permute-start) | collective-permute-done | bytes 524320 | tf_op jit(solution)/shard_map/ppermute | solution.py:91
  13.8 0.7 %collective-permute-done.1.v1_ref = bf16[2048,128]{1,0:T(8,128)(2,1)S(1)} collective-permute-done((bf16[2048,128]{1,0:T(8,128)(2,1)}, bf16[2048,128]{1,0:T(8,128)(2,1)S(1)}, u32[]{:S(2)}, u32[]{:S(2)}) %collective-permute-start.1) | collective-permute-done | bytes 524320 | tf_op jit(solution)/shard_map/ppermute | solution.py:92
  14.6 10.9 %all-to-all-done = bf16[16,80,128]{2,1,0:T(8,128)(2,1)S(1)} async-done(((bf16[16,80,128]{2,1,0:T(8,128)(2,1)}), bf16[16,80,128]{2,1,0:T(8,128)(2,1)S(1)}, u32[]{:S(2)}, u32[]{:S(2)}) %all-to-all-start) | async-done | bytes 327712 | tf_op jit(solution)/shard_map/all_to_all | solution.py:95
  25.5 0.0 copy-start.1
  25.5 1.0 %copy-done.1 = bf16[2048,1,128]{2,0,1:T(8,128)(2,1)S(1)} copy-done((bf16[2048,1,128]{2,0,1:T(8,128)(2,1)S(1)}, bf16[2048,1,128]{2,0,1:T(8,128)(2,1)}, u32[]{:S(2)}) %copy-start.1) | copy-done | bytes 524312
  26.6 0.0 copy-start.2
  26.6 1.0 %copy-done.2 = bf16[2048,1,128]{2,0,1:T(8,128)(2,1)S(1)} copy-done((bf16[2048,1,128]{2,0,1:T(8,128)(2,1)S(1)}, bf16[2048,1,128]{2,0,1:T(8,128)(2,1)}, u32[]{:S(2)}) %copy-start.2) | copy-done | bytes 524312
  27.6 6.0 %read_document.1 = bf16[1280,128]{1,0:T(8,128)(2,1)S(1)} custom-call(bf16[1280,128]{1,0:T(8,128)(2,1)S(1)} %bitcast.7, bf16[2048,128]{1,0:T(8,128)(2,1)S(1)} %bitcast.10, bf16[2048,128]{1,0:T(8,128)(2,1)S(1)} %collective-permute-done.k1_ref, bf16[2048,128]{1,0:T(8,128)(2,1)S(1)} %bitcast.12, bf16[2048,128]{1,0:T(8,128)(2,1)S(1)} %collective-permute-done.1.v1_ref), custom_call_target="tpu_custom_call" | custom-call | tf_op jit(solution)/shard_map/read_document/pallas_call | solution.py:41
  33.7 17.0 %all_to_all.15.parts_ref = bf16[16,80,128]{2,1,0:T(8,128)(2,1)S(1)} all-to-all(bf16[16,80,128]{2,1,0:T(8,128)(2,1)S(1)} %bitcast.8), channel_id=1, replica_groups={{0,16,32,48,64,80,96,112,128,144,160,176,192,208,224,240},{8,24,40,56,7..., dimensions={0} | all-to-all | bytes 655360 | tf_op jit(solution)/shard_map/all_to_all | solution.py:101
  50.7 0.0 copy-start
  50.7 2.9 %copy-done = bf16[640,5120]{1,0:T(8,128)(2,1)S(1)} copy-done((bf16[640,5120]{1,0:T(8,128)(2,1)S(1)}, bf16[640,5120]{1,0:T(8,128)(2,1)}, u32[]{:S(2)}) %copy-start) | copy-done | bytes 6553624
  53.6 0.0 copy-start.3
  53.6 0.7 %copy-done.3 = f32[5,128]{1,0:T(8,128)S(1)} copy-done((f32[5,128]{1,0:T(8,128)S(1)}, f32[5,128]{1,0:T(8,128)}, u32[]{:S(2)}) %copy-start.3) | copy-done | bytes 2584
  54.2 1.1 %project.1 = bf16[8,16,640]{2,1,0:T(8,128)(2,1)S(1)} custom-call(bf16[16,80,128]{2,1,0:T(8,128)(2,1)S(1)} %all_to_all.15.parts_ref, f32[5,128]{1,0:T(8,128)S(1)} %copy-done.3, bf16[640,5120]{1,0:T(8,128)(2,1)S(1)} %copy-done), custom_call_target="tpu_custom_call" | custom-call | tf_op jit(solution)/shard_map/project/pallas_call | solution.py:72
  55.3 11.3 %all_to_all.16 = bf16[8,16,640]{2,1,0:T(8,128)(2,1)S(1)} all-to-all(bf16[8,16,640]{2,1,0:T(8,128)(2,1)S(1)} %project.1), channel_id=1, replica_groups=mesh['seq'=32,'head'=8] {'head'}, dimensions={0} | all-to-all | bytes 327680 | tf_op jit(solution)/shard_map/all_to_all | solution.py:103
  66.6 0.6 reduce_sum.12
Async XLA Ops:
  1.5 24.0 %all-to-all-start = ((bf16[16,80,128]{2,1,0:T(8,128)(2,1)}), bf16[16,80,128]{2,1,0:T(8,128)(2,1)S(1)}, u32[]{:S(2)}, u32[]{:S(2)}) async-start(bf16[16,80,128]{2,1,0:T(8,128)(2,1)} %broadcast_in_dim.8), calls=%async_computation | async-start | bytes 655360 | tf_op jit(solution)/shard_map/all_to_all | solution.py:95
  11.6 2.2 %collective-permute-start = (bf16[2048,128]{1,0:T(8,128)(2,1)}, bf16[2048,128]{1,0:T(8,128)(2,1)S(1)}, u32[]{:S(2)}, u32[]{:S(2)}) collective-permute-start(bf16[2048,128]{1,0:T(8,128)(2,1)} %bitcast.9), channel_id=1, source_target_pairs={{0,8},{8,0},{16,24},{24,16},{32,40},{40,32},{48,56},{56,48},{64,72... | collective-permute-start | bytes 1572872 | tf_op jit(solution)/shard_map/ppermute | solution.py:91
  11.7 2.9 %collective-permute-start.1 = (bf16[2048,128]{1,0:T(8,128)(2,1)}, bf16[2048,128]{1,0:T(8,128)(2,1)S(1)}, u32[]{:S(2)}, u32[]{:S(2)}) collective-permute-start(bf16[2048,128]{1,0:T(8,128)(2,1)} %bitcast.11), channel_id=1, source_target_pairs={{0,8},{8,0},{16,24},{24,16},{32,40},{40,32},{48,56},{56,48},{64,72... | collective-permute-start | bytes 1572872 | tf_op jit(solution)/shard_map/ppermute | solution.py:92
  25.5 1.0 %copy-start.1 = (bf16[2048,1,128]{2,0,1:T(8,128)(2,1)S(1)}, bf16[2048,1,128]{2,0,1:T(8,128)(2,1)}, u32[]{:S(2)}) copy-start(bf16[2048,1,128]{2,0,1:T(8,128)(2,1)} %param.6) | copy-start | bytes 1572868
  26.6 1.0 %copy-start.2 = (bf16[2048,1,128]{2,0,1:T(8,128)(2,1)S(1)}, bf16[2048,1,128]{2,0,1:T(8,128)(2,1)}, u32[]{:S(2)}) copy-start(bf16[2048,1,128]{2,0,1:T(8,128)(2,1)} %param.7) | copy-start | bytes 1572868
  50.7 2.9 %copy-start = (bf16[640,5120]{1,0:T(8,128)(2,1)S(1)}, bf16[640,5120]{1,0:T(8,128)(2,1)}, u32[]{:S(2)}) copy-start(bf16[640,5120]{1,0:T(8,128)(2,1)} %weight_ref.1) | copy-start | bytes 19660804
  53.6 0.7 %copy-start.3 = (f32[5,128]{1,0:T(8,128)S(1)}, f32[5,128]{1,0:T(8,128)}, u32[]{:S(2)}) copy-start(f32[5,128]{1,0:T(8,128)} %gain_ref.1) | copy-start | bytes 7684

commit v2 on v1

--- a/solution.py
+++ b/solution.py
@@ -21,10 +21,35 @@
     ]
 
 
-def read_kernel(q_ref, k0_ref, k1_ref, v0_ref, v1_ref, o_ref):
+def read_kernel(
+    q_ref,
+    k_near_ref,
+    v_near_ref,
+    k_hbm,
+    v_hbm,
+    weight_hbm,
+    gain_hbm,
+    o_ref,
+    weight_ref,
+    gain_ref,
+    k_own_ref,
+    v_own_ref,
+    sems,
+):
+    copies = [
+        pltpu.make_async_copy(src, dst, sems.at[i])
+        for i, (src, dst) in enumerate(
+            ((k_hbm, k_own_ref), (v_hbm, v_own_ref), (weight_hbm, weight_ref), (gain_hbm, gain_ref))
+        )
+    ]
+    for copy in copies:
+        copy.start()
     rows = q_ref[...]
     total = None
-    for k_ref, v_ref in ((k0_ref, v0_ref), (k1_ref, v1_ref)):
+    for k_ref, v_ref in ((k_near_ref, v_near_ref), (k_own_ref, v_own_ref)):
+        if k_ref is k_own_ref:
+            copies[0].wait()
+            copies[1].wait()
         for start in range(0, k_ref.shape[0], KEY_TILE):
             tile = pl.ds(start, KEY_TILE)
             scores = lax.dot_general(
@@ -34,18 +59,34 @@
             term = jnp.dot(weights, v_ref[tile, :], preferred_element_type=jnp.float32)
             total = term if total is None else total + term
     o_ref[...] = total.astype(o_ref.dtype)
+    copies[2].wait()
+    copies[3].wait()
 
 
-def read_document(rows, keys, values):
+def read_document(rows, near, own, weight, gain):
     vmem = pl.BlockSpec(memory_space=pltpu.VMEM)
+    hbm = pl.BlockSpec(memory_space=pltpu.HBM)
     return pl.pallas_call(
         read_kernel,
-        out_shape=jax.ShapeDtypeStruct(rows.shape, jnp.bfloat16),
-        in_specs=[vmem] * 5,
-        out_specs=vmem,
-        compiler_params=pltpu.CompilerParams(vmem_limit_bytes=24 << 20),
+        out_shape=(
+            jax.ShapeDtypeStruct(rows.shape, jnp.bfloat16),
+            jax.ShapeDtypeStruct(weight.shape, weight.dtype),
+            jax.ShapeDtypeStruct(gain.shape, gain.dtype),
+        ),
+        in_specs=[vmem] * 3 + [hbm] * 4,
+        out_specs=(vmem, vmem, vmem),
+        scratch_shapes=[
+            pltpu.VMEM(own[0].shape, own[0].dtype),
+            pltpu.VMEM(own[1].shape, own[1].dtype),
+            pltpu.SemaphoreType.DMA((4,)),
+        ],
+        compiler_params=pltpu.CompilerParams(vmem_limit_bytes=32 << 20),
         name="read_document",
-    )(rows, *keys, *values)
+    )(
+        rows,
+        *near,
+        *(pltpu.with_memory_space_constraint(a, pltpu.HBM) for a in (*own, weight, gain)),
+    )
 
 
 def project_kernel(parts_ref, gain_ref, weight_ref, o_ref):
@@ -93,13 +134,16 @@
     own = jnp.transpose(queries, (1, 0, 2)).reshape(heads * rows, width)
     copies = jnp.broadcast_to(own[None], (peer_count, heads * rows, width))
     gathered = lax.all_to_all(copies, "seq", 0, 0, axis_index_groups=peers, tiled=True)
-    partial = read_document(
+    partial, weight, gain = read_document(
         gathered.reshape(peer_count * heads * rows, width),
-        (keys, other_keys),
-        (values, other_values),
-    ).reshape(peer_count, heads * rows, width)
+        (other_keys, other_values),
+        (keys, values),
+        out_weight,
+        out_gain,
+    )
+    partial = partial.reshape(peer_count, heads * rows, width)
     parts = lax.all_to_all(partial, "seq", 0, 0, axis_index_groups=peers, tiled=True)
-    projected = project(parts, out_gain, out_weight, head_groups)
+    projected = project(parts, gain, weight, head_groups)
     pieces = lax.all_to_all(projected, "head", 0, 0, tiled=True)
     return jnp.sum(pieces.astype(jnp.float32), axis=0).astype(jnp.bfloat16)
 

time: 67.7 us -> 63.1 us (0.932)
  local copies, waits for them, and re-layouts: 7.12 us -> 1.49 us
  Pallas kernels: 7.11 us -> 8.29 us
    unnamed x8 -> x0, local copies, waits for them, and re-layouts: 5.63 us -> none
    pallas_call x1, Pallas kernels: 6.04 us -> 7.21 us  [read_document(): pl.pallas_call(read_kernel, out_shape=(jax.ShapeDtypeStruct(rows.shape, j...]
where the time goes in v2:
time: 63.1 us; the launch traced here: 62.8 us
  blocking collectives  28.3 us (45%)
  waiting for transfers between devices  13.3 us (21%)
  starting transfers between devices  10.7 us (17%)
  Pallas kernels  8.29 us (13%)
  local copies, waits for them, and re-layouts  1.49 us (2%)
    all_to_all x1, blocking collectives, on_device(): lax.all_to_all(partial, 'seq', 0, 0, axis_index_groups=peers, tiled=True)  17.1 us
    all_to_all x1, blocking collectives, on_device(): pieces = lax.all_to_all(projected, 'head', 0, 0, tiled=True)  11.3 us
    all_to_all x1, waiting for transfers between devices, on_device(): lax.all_to_all(copies, 'seq', 0, 0, axis_index_groups=peers, tiled=True)  10.9 us
    all_to_all x1, starting transfers between devices, on_device(): lax.all_to_all(copies, 'seq', 0, 0, axis_index_groups=peers, tiled=True)  10.1 us
    pallas_call x1, Pallas kernels, read_document(): pl.pallas_call(read_kernel, out_shape=(jax.ShapeDtypeStruct(rows.shape, j...  7.21 us
    ppermute x1, waiting for transfers between devices, on_device(): other_keys = lax.ppermute(keys, 'seq', other_core)  1.61 us
    broadcast_in_dim x1, local copies, waits for them, and re-layouts, on_device(): copies = jnp.broadcast_to(own[None], (peer_count, heads * rows, width))  1.49 us
  transfers between devices with their start and end apart: 3, of which 3 were waited for; matrix products, arithmetic and copies ran while one was open for 0% of the time, Pallas kernels for 0%

profile of v2, /device:TPU:32, one launch (start us, length us, event | category | flops | bytes accessed | tf_op | source)
XLA Modules:
  0.0 62.8 jit_solution(654185666487297423)
XLA Ops:
  0.0 1.5 %broadcast_in_dim.8 = bf16[16,80,128]{2,1,0:T(8,128)(2,1)} broadcast(bf16[80,128]{1,0:T(8,128)(2,1)} %bitcast.13), dimensions={1,2} | broadcast | bytes 348160 | tf_op jit(solution)/shard_map/broadcast_in_dim | solution.py:135
  1.5 10.1 %all-to-all-start = ((bf16[16,80,128]{2,1,0:T(8,128)(2,1)}), bf16[16,80,128]{2,1,0:T(8,128)(2,1)S(1)}, u32[]{:S(2)}, u32[]{:S(2)}) async-start(bf16[16,80,128]{2,1,0:T(8,128)(2,1)} %broadcast_in_dim.8), calls=%async_computation | async-start | bytes 655360 | tf_op jit(solution)/shard_map/all_to_all | solution.py:136
  11.6 0.1 collective-permute-start
  11.7 0.5 collective-permute-start.1
  12.2 1.6 %collective-permute-done.k_near_ref = bf16[2048,128]{1,0:T(8,128)(2,1)S(1)} collective-permute-done((bf16[2048,128]{1,0:T(8,128)(2,1)}, bf16[2048,128]{1,0:T(8,128)(2,1)S(1)}, u32[]{:S(2)}, u32[]{:S(2)}) %collective-permute-start) | collective-permute-done | bytes 524320 | tf_op jit(solution)/shard_map/ppermute | solution.py:132
  13.8 0.7 %collective-permute-done.1.v_near_ref = bf16[2048,128]{1,0:T(8,128)(2,1)S(1)} collective-permute-done((bf16[2048,128]{1,0:T(8,128)(2,1)}, bf16[2048,128]{1,0:T(8,128)(2,1)S(1)}, u32[]{:S(2)}, u32[]{:S(2)}) %collective-permute-start.1) | collective-permute-done | bytes 524320 | tf_op jit(solution)/shard_map/ppermute | solution.py:133
  14.6 10.9 %all-to-all-done = bf16[16,80,128]{2,1,0:T(8,128)(2,1)S(1)} async-done(((bf16[16,80,128]{2,1,0:T(8,128)(2,1)}), bf16[16,80,128]{2,1,0:T(8,128)(2,1)S(1)}, u32[]{:S(2)}, u32[]{:S(2)}) %all-to-all-start) | async-done | bytes 327712 | tf_op jit(solution)/shard_map/all_to_all | solution.py:136
  25.5 7.2 %read_document.1 = (bf16[1280,128]{1,0:T(8,128)(2,1)S(1)}, bf16[640,5120]{1,0:T(8,128)(2,1)S(1)}, f32[5,128]{1,0:T(8,128)S(1)}) custom-call(bf16[1280,128]{1,0:T(8,128)(2,1)S(1)} %bitcast.7, bf16[2048,128]{1,0:T(8,128)(2,1)S(1)} %collective-permute-done.k_near_ref, bf16[2048,128]{1,0:T(8,128)(2,1)S(1)} %collective-permute-done.1.v_near_ref, ...), custom_call_target="tpu_custom_call" | custom-call | tf_op jit(solution)/shard_map/read_document/pallas_call | solution.py:69
  32.7 17.1 %all_to_all.15.parts_ref = bf16[16,80,128]{2,1,0:T(8,128)(2,1)S(1)} all-to-all(bf16[16,80,128]{2,1,0:T(8,128)(2,1)S(1)} %bitcast.8), channel_id=1, replica_groups={{0,16,32,48,64,80,96,112,128,144,160,176,192,208,224,240},{8,24,40,56,7..., dimensions={0} | all-to-all | bytes 655360 | tf_op jit(solution)/shard_map/all_to_all | solution.py:145
  49.8 1.1 %project.1 = bf16[8,16,640]{2,1,0:T(8,128)(2,1)S(1)} custom-call(bf16[16,80,128]{2,1,0:T(8,128)(2,1)S(1)} %all_to_all.15.parts_ref, f32[5,128]{1,0:T(8,128)S(1)} %get-tuple-element.9.gain_ref, bf16[640,5120]{1,0:T(8,128)(2,1)S(1)} %get-tuple-element.10.weight_ref), custom_call_target="tpu_custom_call" | custom-call | tf_op jit(solution)/shard_map/project/pallas_call | solution.py:113
  50.9 11.3 %all_to_all.16 = bf16[8,16,640]{2,1,0:T(8,128)(2,1)S(1)} all-to-all(bf16[8,16,640]{2,1,0:T(8,128)(2,1)S(1)} %project.1), channel_id=1, replica_groups=mesh['seq'=32,'head'=8] {'head'}, dimensions={0} | all-to-all | bytes 327680 | tf_op jit(solution)/shard_map/all_to_all | solution.py:147
  62.2 0.6 %reduce_sum.12 = bf16[16,640]{1,0:T(8,128)(2,1)} reduce(bf16[8,16,640]{2,1,0:T(8,128)(2,1)S(1)} %all_to_all.16, bf16[]{:T(256)} %constant.2.clone.1), dimensions={0}, to_apply=%region_0.0 | reduce | flops 71680 | bytes 184322 | tf_op jit(solution)/shard_map/reduce_sum | solution.py:148
Async XLA Ops:
  1.5 24.0 %all-to-all-start = ((bf16[16,80,128]{2,1,0:T(8,128)(2,1)}), bf16[16,80,128]{2,1,0:T(8,128)(2,1)S(1)}, u32[]{:S(2)}, u32[]{:S(2)}) async-start(bf16[16,80,128]{2,1,0:T(8,128)(2,1)} %broadcast_in_dim.8), calls=%async_computation | async-start | bytes 655360 | tf_op jit(solution)/shard_map/all_to_all | solution.py:136
  11.6 2.2 %collective-permute-start = (bf16[2048,128]{1,0:T(8,128)(2,1)}, bf16[2048,128]{1,0:T(8,128)(2,1)S(1)}, u32[]{:S(2)}, u32[]{:S(2)}) collective-permute-start(bf16[2048,128]{1,0:T(8,128)(2,1)} %bitcast.9), channel_id=1, source_target_pairs={{0,8},{8,0},{16,24},{24,16},{32,40},{40,32},{48,56},{56,48},{64,72... | collective-permute-start | bytes 1572872 | tf_op jit(solution)/shard_map/ppermute | solution.py:132
  11.7 2.9 %collective-permute-start.1 = (bf16[2048,128]{1,0:T(8,128)(2,1)}, bf16[2048,128]{1,0:T(8,128)(2,1)S(1)}, u32[]{:S(2)}, u32[]{:S(2)}) collective-permute-start(bf16[2048,128]{1,0:T(8,128)(2,1)} %bitcast.11), channel_id=1, source_target_pairs={{0,8},{8,0},{16,24},{24,16},{32,40},{40,32},{48,56},{56,48},{64,72... | collective-permute-start | bytes 1572872 | tf_op jit(solution)/shard_map/ppermute | solution.py:133

commit v3 on v1

v3 whole, which is shorter than its diff:
```python
import functools

import jax
import jax.numpy as jnp
from jax import lax
from jax.experimental import pallas as pl
from jax.experimental.pallas import tpu as pltpu
from jax.sharding import PartitionSpec as P

CONTRACT_LAST = (((1,), (1,)), ((), ()))
KEY_TILE = 256
X_CHIPS, Z_BLOCKS, CORES = 4, 4, 2
ORDER = (2, 3, 1)


def seq_index(z_block, x_chip, core):
    return (z_block * X_CHIPS + x_chip) * CORES + core


def exchange(rows, z_step, x_step, core_step):
    pairs = []
    for z in range(Z_BLOCKS):
        for x in range(X_CHIPS):
            for core in range(CORES):
                to = seq_index(z ^ z_step, x ^ x_step, core ^ core_step)
                pairs.append((seq_index(z, x, core), to))
    return lax.ppermute(rows, "seq", pairs)


VMEM = pl.BlockSpec(memory_space=pltpu.VMEM)
HBM = pl.BlockSpec(memory_space=pltpu.HBM)


def in_hbm(array):
    return pltpu.with_memory_space_constraint(array, pltpu.HBM)


def params(mib):
    return pltpu.CompilerParams(vmem_limit_bytes=mib << 20)


def stage_kernel(*refs):
    count = len(refs) // 2
    copies = []
    for i in range(count):
        source, target = refs[i], refs[count + i]
        if source.shape != target.shape:
            source = source.at[pl.ds(0, target.shape[0]), :]
        copies.append(pltpu.make_async_copy(source, target, refs[-1].at[i]))
    for copy in copies:
        copy.start()
    for copy in copies:
        copy.wait()


def stage(*arrays, row_counts):
    return pl.pallas_call(
        stage_kernel,
        out_shape=tuple(
            jax.ShapeDtypeStruct((count,) + a.shape[1:], a.dtype)
            for a, count in zip(arrays, row_counts)
        ),
        in_specs=[HBM] * len(arrays),
        out_specs=(VMEM,) * len(arrays),
        scratch_shapes=[pltpu.SemaphoreType.DMA((len(arrays),))],
        compiler_params=params(4),
        cost_estimate=pl.CostEstimate(flops=0, bytes_accessed=4 << 20, transcendentals=0),
        name="stage",
    )(*(in_hbm(a) for a in arrays))


def join_kernel(*refs):
    for i, ref in enumerate(refs[:-1]):
        refs[-1][i] = ref[...]


def join(arrays):
    shape = (len(arrays),) + arrays[0].shape
    return pl.pallas_call(
        join_kernel,
        out_shape=jax.ShapeDtypeStruct(shape, arrays[0].dtype),
        in_specs=[VMEM] * len(arrays),
        out_specs=VMEM,
        compiler_params=params(2),
        name="join",
    )(*arrays)


def read_rows(q_ref, pairs, o_ref):
    chunks, count, width = q_ref.shape
    rows = q_ref[...].reshape(chunks * count, width)
    total = None
    for k_ref, v_ref in pairs:
        for start in range(0, k_ref.shape[0], KEY_TILE):
            tile = pl.ds(start, KEY_TILE)
            scores = lax.dot_general(
                rows, k_ref[tile, :], CONTRACT_LAST, preferred_element_type=jnp.float32
            )
            weights = (scores * scores).astype(jnp.bfloat16)
            term = jnp.dot(weights, v_ref[tile, :], preferred_element_type=jnp.float32)
            total = term if total is None else total + term
    o_ref[...] = total.astype(o_ref.dtype).reshape(q_ref.shape)


def read_kernel(q_ref, k0_ref, v0_ref, k1_ref, v1_ref, after_ref, o_ref):
    read_rows(q_ref, ((k0_ref, v0_ref), (k1_ref, v1_ref)), o_ref)


def read(rows, document, after):
    tokens = sum(a.shape[0] for a in document) // 2
    size = rows.shape[0] * rows.shape[1]
    return pl.pallas_call(
        read_kernel,
        out_shape=jax.ShapeDtypeStruct(rows.shape, jnp.bfloat16),
        in_specs=[VMEM] * 5 + [pl.BlockSpec(memory_space=pl.ANY)],
        out_specs=VMEM,
        compiler_params=params(16),
        cost_estimate=pl.CostEstimate(
            flops=4 * size * tokens * rows.shape[2], bytes_accessed=4 << 20, transcendentals=0
        ),
        name="read",
    )(rows, *document, after)


def fetch_kernel(first_row, w_hbm, w_ref, sem):
    copy = pltpu.make_async_copy(w_hbm.at[pl.ds(first_row, w_ref.shape[0]), :], w_ref, sem)
    copy.start()
    copy.wait()


def fetch(weight, first_row, row_count):
    return pl.pallas_call(
        functools.partial(fetch_kernel, first_row),
        out_shape=jax.ShapeDtypeStruct((row_count, weight.shape[1]), weight.dtype),
        in_specs=[HBM],
        out_specs=VMEM,
        scratch_shapes=[pltpu.SemaphoreType.DMA],
        compiler_params=params(2),
        cost_estimate=pl.CostEstimate(flops=0, bytes_accessed=4 << 20, transcendentals=0),
        name="fetch",
    )(in_hbm(weight))


def add_kernel(*refs):
    count = refs[0].shape[0]
    for slot in range(count):
        total = refs[0][slot].astype(jnp.float32)
        for ref in refs[1:-count]:
            total = total + ref[slot].astype(jnp.float32)
        refs[slot - count][...] = total.astype(refs[slot - count].dtype)


def add(parts):
    count = parts[0].shape[0]
    out = jax.ShapeDtypeStruct(parts[0].shape[1:], parts[0].dtype)
    return pl.pallas_call(
        add_kernel,
        out_shape=(out,) * count,
        in_specs=[VMEM] * len(parts),
        out_specs=(VMEM,) * count,
        compiler_params=params(4),
        name="add",
    )(*parts)


def project_kernel(part_count, *refs):
    part_refs, gain_ref, o_ref = refs[:part_count], refs[part_count], refs[-1]
    weight_refs = refs[part_count + 1 : -1]
    retained = part_refs[0][...].astype(jnp.float32)
    for part_ref in part_refs[1:]:
        retained = retained + part_ref[...].astype(jnp.float32)
    heads, _ = gain_ref.shape
    rows = retained.shape[0] // heads
    pieces = []
    for h in range(heads):
        one = retained[h * rows : (h + 1) * rows, :]
        mean_square = jnp.mean(one * one, axis=-1, keepdims=True)
        normed = one * lax.rsqrt(mean_square + 1e-06) * gain_ref[pl.ds(h, 1), :]
        pieces.append(normed.astype(jnp.bfloat16))
    flat = jnp.concatenate(pieces, axis=1)
    chunk = o_ref.shape[2]
    for g in range(o_ref.shape[0]):
        total, first = None, 0
        for weight_ref in weight_refs:
            last = first + weight_ref.shape[0]
            term = jnp.dot(
                flat[:, first:last],
                weight_ref[:, g * chunk : (g + 1) * chunk],
                preferred_element_type=jnp.float32,
            )
            total, first = term if total is None else total + term, last
        o_ref[g] = total.astype(o_ref.dtype)


def project(parts, gain, weights, groups):
    rows = parts[0].shape[0] // gain.shape[0]
    return pl.pallas_call(
        functools.partial(project_kernel, len(parts)),
        out_shape=jax.ShapeDtypeStruct((groups, rows, weights[0].shape[1] // groups), jnp.bfloat16),
        in_specs=[VMEM] * (len(parts) + 1 + len(weights)),
        out_specs=VMEM,
        compiler_params=params(24),
        name="project",
    )(*parts, gain, *weights)


def layer(queries, document_key_rows, document_value_rows, out_gain, out_weight):
    rows, heads, width = queries.shape
    tokens = document_key_rows.shape[0]
    head_groups = lax.axis_size("head")
    keys = document_key_rows.reshape(tokens, width)
    values = document_value_rows.reshape(tokens, width)
    own = jnp.transpose(queries, (1, 0, 2)).reshape(heads * rows, width)
    from_z = {}
    for steps in ORDER:
        from_z[steps] = exchange(own, steps, 0, steps >> 1)
    other_core = [(i, i ^ 1) for i in range(lax.axis_size("seq"))]
    near_keys = lax.ppermute(keys, "seq", other_core)
    near_values = lax.ppermute(values, "seq", other_core)
    staged_own, staged_keys, staged_values, gain, weight = stage(
        own,
        keys,
        values,
        out_gain,
        out_weight,
        row_counts=(heads * rows, tokens, tokens, heads, width),
    )
    column = join([staged_own, *(from_z[steps] for steps in range(1, Z_BLOCKS))])
    document = (staged_keys, staged_values, near_keys, near_values)
    from_x = {}
    for steps in ORDER:
        from_x[steps] = exchange(column, 0, steps, 1)
    part, parts = staged_own, []
    for steps in (0, *ORDER):
        part = read(from_x[steps] if steps else column, document, part)
        parts.append(exchange(part, 0, steps, 1) if steps else part)
    middle = width * (1 + (heads - 1) // 2)
    middle_weight = fetch(out_weight, width, middle - width)
    last_weight = fetch(out_weight, middle, heads * width - middle)
    weights = [weight, middle_weight, last_weight]
    slots = add(parts)
    parts = [slots[0]]
    for steps in ORDER:
        parts.append(exchange(slots[steps], steps, 0, steps >> 1))
    projected = project(parts, gain, weights, head_groups)
    pieces = lax.all_to_all(projected, "head", 0, 0, tiled=True)
    return jnp.sum(pieces.astype(jnp.float32), axis=0).astype(jnp.bfloat16)


def solution(mesh):
    in_specs = (
        P("seq", "head", None),
        P("seq", "head", None),
        P("seq", "head", None),
        P("head", None),
        P("head", None),
    )
    out_specs = P("seq", "head")
    return jax.shard_map(layer, mesh=mesh, in_specs=in_specs, out_specs=out_specs, check_vma=False)
```

time: 67.7 us -> 57.4 us (0.85)
  blocking collectives: 28.3 us -> 11.7 us
  starting transfers between devices: 10.7 us -> 22.2 us
  local copies, waits for them, and re-layouts: 7.12 us -> 0 us
  Pallas kernels: 7.11 us -> 13.2 us
  waiting for transfers between devices: 13.3 us -> 8.44 us
    ppermute x2 -> x14, starting transfers between devices: 0.59 us -> 22.2 us  [the longest x12 21.7 us: exchange(): return lax.ppermute(rows, 'seq', pairs)]
    all_to_all x2 -> x1, blocking collectives: 28.3 us -> 11.7 us  [layer(): pieces = lax.all_to_all(projected, 'head', 0, 0, tiled=True)]
    all_to_all x1 -> x0, waiting for transfers between devices: 10.9 us -> none  [on_device(): lax.all_to_all(copies, 'seq', 0, 0, axis_index_groups=peers, tiled=True)]
    all_to_all x1 -> x0, starting transfers between devices: 10.1 us -> none  [on_device(): lax.all_to_all(copies, 'seq', 0, 0, axis_index_groups=peers, tiled=True)]
    ppermute x2 -> x14, waiting for transfers between devices: 2.36 us -> 8.44 us  [the longest x12 8.44 us: exchange(): return lax.ppermute(rows, 'seq', pairs)]
    pallas_call x2 -> x10, Pallas kernels: 7.11 us -> 13.2 us  [the longest x4 6.84 us: read(): pl.pallas_call(read_kernel, out_shape=jax.ShapeDtypeStruct(rows.shape, jn...]
    unnamed x8 -> x0, local copies, waits for them, and re-layouts: 5.63 us -> none
    broadcast_in_dim x1 -> x0, local copies, waits for them, and re-layouts: 1.49 us -> none  [on_device(): copies = jnp.broadcast_to(own[None], (peer_count, heads * rows, width))]
  transfers between devices with their start and end apart: 3 -> 14, of which waited for: 3 -> 6; matrix products, arithmetic and copies ran while one was open for 0% -> 0% of each run, Pallas kernels for 0% -> 18%
where the time goes in v3:
time: 57.4 us; the launch traced here: 56.3 us
  starting transfers between devices  22.2 us (39%)
  Pallas kernels  13.2 us (23%)
  blocking collectives  11.7 us (20%)
  waiting for transfers between devices  8.44 us (15%)
  other arithmetic  0.63 us (1%)
    ppermute x12, starting transfers between devices, exchange(): return lax.ppermute(rows, 'seq', pairs)  21.7 us
    all_to_all x1, blocking collectives, layer(): pieces = lax.all_to_all(projected, 'head', 0, 0, tiled=True)  11.7 us
    ppermute x12, waiting for transfers between devices, exchange(): return lax.ppermute(rows, 'seq', pairs)  8.44 us
    pallas_call x4, Pallas kernels, read(): pl.pallas_call(read_kernel, out_shape=jax.ShapeDtypeStruct(rows.shape, jn...  6.84 us
    pallas_call x2, Pallas kernels, fetch(): pl.pallas_call(functools.partial(fetch_kernel, first_row), out_shape=jax....  3.5 us
    pallas_call x1, Pallas kernels, stage(): pl.pallas_call(stage_kernel, out_shape=tuple((jax.ShapeDtypeStruct((count...  1.71 us
  transfers between devices with their start and end apart: 14, of which 6 were waited for; matrix products, arithmetic and copies ran while one was open for 0% of the time, Pallas kernels for 18%

profile of v3, /device:TPU:32, one launch (start us, length us, event | category | flops | bytes accessed | tf_op | source)
XLA Modules:
  0.0 56.3 jit_solution(11349609666039582537)
XLA Ops:
  0.5 5.0 %collective-permute-start.2 = (bf16[80,128]{1,0:T(8,128)(2,1)}, bf16[80,128]{1,0:T(8,128)(2,1)S(1)}, u32[]{:S(2)}, u32[]{:S(2)}) collective-permute-start(bf16[80,128]{1,0:T(8,128)(2,1)} %bitcast.9), channel_id=1, source_target_pairs={{0,200},{8,192},{16,216},{24,208},{32,232},{40,224},{48,248},{56,2... | collective-permute-start | bytes 61448 | tf_op jit(solution)/shard_map/ppermute | solution.py:27
  5.5 1.6 %collective-permute-start.1 = (bf16[80,128]{1,0:T(8,128)(2,1)}, bf16[80,128]{1,0:T(8,128)(2,1)S(1)}, u32[]{:S(2)}, u32[]{:S(2)}) collective-permute-start(bf16[80,128]{1,0:T(8,128)(2,1)} %bitcast.10), channel_id=1, source_target_pairs={{0,136},{8,128},{16,152},{24,144},{32,168},{40,160},{48,184},{56,1... | collective-permute-start | bytes 61448 | tf_op jit(solution)/shard_map/ppermute | solution.py:27
  7.1 0.8 %collective-permute-start = (bf16[80,128]{1,0:T(8,128)(2,1)}, bf16[80,128]{1,0:T(8,128)(2,1)S(1)}, u32[]{:S(2)}, u32[]{:S(2)}) collective-permute-start(bf16[80,128]{1,0:T(8,128)(2,1)} %bitcast.11), channel_id=1, source_target_pairs={{0,64},{8,72},{16,80},{24,88},{32,96},{40,104},{48,112},{56,120},{... | collective-permute-start | bytes 61448 | tf_op jit(solution)/shard_map/ppermute | solution.py:27
  7.9 1.7 %stage.1 = (bf16[80,128]{1,0:T(8,128)(2,1)S(1)}, bf16[2048,128]{1,0:T(8,128)(2,1)S(1)}, bf16[2048,128]{1,0:T(8,128)(2,1)S(1)}, f32[5,128]{1,0:T(8,128)S(1)}, bf16[128,5120]{1,0:T(8,128)(2,1)S(1)}) custom-call(bf16[80,128]{1,0:T(8,128)(2,1)} %bitcast.12, bf16[2048,128]{1,0:T(8,128)(2,1)} %bitcast.6, bf16[2048,128]{1,0:T(8,128)(2,1)} %bitcast.8, ...), custom_call_target="tpu_custom_call" | custom-call | bytes 4194304 | tf_op jit(solution)/shard_map/stage/pallas_call | solution.py:57
  9.6 3.2 %collective-permute-done.1.refs_2_ = bf16[80,128]{1,0:T(8,128)(2,1)S(1)} collective-permute-done((bf16[80,128]{1,0:T(8,128)(2,1)}, bf16[80,128]{1,0:T(8,128)(2,1)S(1)}, u32[]{:S(2)}, u32[]{:S(2)}) %collective-permute-start.1) | collective-permute-done | bytes 20512 | tf_op jit(solution)/shard_map/ppermute | solution.py:27
  12.9 3.2 %collective-permute-start.5 = (bf16[4,80,128]{2,1,0:T(8,128)(2,1)S(1)}, bf16[4,80,128]{2,1,0:T(8,128)(2,1)S(1)}, u32[]{:S(2)}, u32[]{:S(2)}) collective-permute-start(bf16[4,80,128]{2,1,0:T(8,128)(2,1)S(1)} %join.1.q_ref), channel_id=1, source_target_pairs={{0,40},{8,32},{16,56},{24,48},{32,8},{40,0},{48,24},{56,16},{64,10... | collective-permute-start | bytes 245768 | tf_op jit(solution)/shard_map/ppermute | solution.py:27
  16.9 1.7 %read.4.after_ref.refs_0_ = bf16[4,80,128]{2,1,0:T(8,128)(2,1)S(1)} custom-call(bf16[4,80,128]{2,1,0:T(8,128)(2,1)S(1)} %join.1.q_ref, bf16[2048,128]{1,0:T(8,128)(2,1)S(1)} %get-tuple-element.15.k0_ref, bf16[2048,128]{1,0:T(8,128)(2,1)S(1)} %get-tuple-element.16.v0_ref, bf16[2048,128]{1,0:T(8,128)(2,1)S(1)} %collective-permute-done.3.k1_ref, ...), custom_call_target="tpu_custom_call" | custom-call | flops 671088640 | bytes 4194304 | tf_op jit(solution)/shard_map/read/pallas_call | solution.py:112
  18.9 1.7 %read.5.after_ref = bf16[4,80,128]{2,1,0:T(8,128)(2,1)S(1)} custom-call(bf16[4,80,128]{2,1,0:T(8,128)(2,1)S(1)} %collective-permute-done.5.q_ref, bf16[2048,128]{1,0:T(8,128)(2,1)S(1)} %get-tuple-element.15.k0_ref, bf16[2048,128]{1,0:T(8,128)(2,1)S(1)} %get-tuple-element.16.v0_ref, bf16[2048,128]{1,0:T(8,128)(2,1)S(1)} %collective-permute-done.3.k1_ref, ...), custom_call_target="tpu_custom_call" | custom-call | flops 671088640 | bytes 4194304 | tf_op jit(solution)/shard_map/read/pallas_call | solution.py:112
  20.6 0.9 %collective-permute-done.7.q_ref = bf16[4,80,128]{2,1,0:T(8,128)(2,1)S(1)} collective-permute-done((bf16[4,80,128]{2,1,0:T(8,128)(2,1)S(1)}, bf16[4,80,128]{2,1,0:T(8,128)(2,1)S(1)}, u32[]{:S(2)}, u32[]{:S(2)}) %collective-permute-start.7) | collective-permute-done | bytes 81952 | tf_op jit(solution)/shard_map/ppermute | solution.py:27
  21.5 1.7 %read.6.after_ref = bf16[4,80,128]{2,1,0:T(8,128)(2,1)S(1)} custom-call(bf16[4,80,128]{2,1,0:T(8,128)(2,1)S(1)} %collective-permute-done.7.q_ref, bf16[2048,128]{1,0:T(8,128)(2,1)S(1)} %get-tuple-element.15.k0_ref, bf16[2048,128]{1,0:T(8,128)(2,1)S(1)} %get-tuple-element.16.v0_ref, bf16[2048,128]{1,0:T(8,128)(2,1)S(1)} %collective-permute-done.3.k1_ref, ...), custom_call_target="tpu_custom_call" | custom-call | flops 671088640 | bytes 4194304 | tf_op jit(solution)/shard_map/read/pallas_call | solution.py:112
  23.3 1.7 %read.7 = bf16[4,80,128]{2,1,0:T(8,128)(2,1)S(1)} custom-call(bf16[4,80,128]{2,1,0:T(8,128)(2,1)S(1)} %collective-permute-done.9.q_ref, bf16[2048,128]{1,0:T(8,128)(2,1)S(1)} %get-tuple-element.15.k0_ref, bf16[2048,128]{1,0:T(8,128)(2,1)S(1)} %get-tuple-element.16.v0_ref, bf16[2048,128]{1,0:T(8,128)(2,1)S(1)} %collective-permute-done.3.k1_ref, ...), custom_call_target="tpu_custom_call" | custom-call | flops 671088640 | bytes 4194304 | tf_op jit(solution)/shard_map/read/pallas_call | solution.py:112
  25.0 1.1 %collective-permute-start.10 = (bf16[4,80,128]{2,1,0:T(8,128)(2,1)S(1)}, bf16[4,80,128]{2,1,0:T(8,128)(2,1)S(1)}, u32[]{:S(2)}, u32[]{:S(2)}) collective-permute-start(bf16[4,80,128]{2,1,0:T(8,128)(2,1)S(1)} %read.7), channel_id=1, source_target_pairs={{0,24},{8,16},{16,8},{24,0},{32,56},{40,48},{48,40},{56,32},{64,88... | collective-permute-start | bytes 245768 | tf_op jit(solution)/shard_map/ppermute | solution.py:27
  26.1 1.5 %collective-permute-start.8 = (bf16[4,80,128]{2,1,0:T(8,128)(2,1)S(1)}, bf16[4,80,128]{2,1,0:T(8,128)(2,1)S(1)}, u32[]{:S(2)}, u32[]{:S(2)}) collective-permute-start(bf16[4,80,128]{2,1,0:T(8,128)(2,1)S(1)} %read.6.after_ref), channel_id=1, source_target_pairs={{0,56},{8,48},{16,40},{24,32},{32,24},{40,16},{48,8},{56,0},{64,12... | collective-permute-start | bytes 245768 | tf_op jit(solution)/shard_map/ppermute | solution.py:27
  27.6 1.4 %collective-permute-start.6 = (bf16[4,80,128]{2,1,0:T(8,128)(2,1)S(1)}, bf16[4,80,128]{2,1,0:T(8,128)(2,1)S(1)}, u32[]{:S(2)}, u32[]{:S(2)}) collective-permute-start(bf16[4,80,128]{2,1,0:T(8,128)(2,1)S(1)} %read.5.after_ref), channel_id=1, source_target_pairs={{0,40},{8,32},{16,56},{24,48},{32,8},{40,0},{48,24},{56,16},{64,10... | collective-permute-start | bytes 245768 | tf_op jit(solution)/shard_map/ppermute | solution.py:27
  29.1 2.9 %collective-permute-done.8.refs_2_ = bf16[4,80,128]{2,1,0:T(8,128)(2,1)S(1)} collective-permute-done((bf16[4,80,128]{2,1,0:T(8,128)(2,1)S(1)}, bf16[4,80,128]{2,1,0:T(8,128)(2,1)S(1)}, u32[]{:S(2)}, u32[]{:S(2)}) %collective-permute-start.8) | collective-permute-done | bytes 81952 | tf_op jit(solution)/shard_map/ppermute | solution.py:27
  32.0 0.9 %collective-permute-done.6.refs_1_ = bf16[4,80,128]{2,1,0:T(8,128)(2,1)S(1)} collective-permute-done((bf16[4,80,128]{2,1,0:T(8,128)(2,1)S(1)}, bf16[4,80,128]{2,1,0:T(8,128)(2,1)S(1)}, u32[]{:S(2)}, u32[]{:S(2)}) %collective-permute-start.6) | collective-permute-done | bytes 81952 | tf_op jit(solution)/shard_map/ppermute | solution.py:27
  33.0 3.7 %collective-permute-start.11 = (bf16[80,128]{1,0:T(8,128)(2,1)S(1)}, bf16[80,128]{1,0:T(8,128)(2,1)S(1)}, u32[]{:S(2)}, u32[]{:S(2)}) collective-permute-start(bf16[80,128]{1,0:T(8,128)(2,1)S(1)} %get-tuple-element.18), channel_id=1, source_target_pairs={{0,136},{8,128},{16,152},{24,144},{32,168},{40,160},{48,184},{56,1... | collective-permute-start | bytes 61448 | tf_op jit(solution)/shard_map/ppermute | solution.py:27
  36.7 1.4 %collective-permute-start.12 = (bf16[80,128]{1,0:T(8,128)(2,1)S(1)}, bf16[80,128]{1,0:T(8,128)(2,1)S(1)}, u32[]{:S(2)}, u32[]{:S(2)}) collective-permute-start(bf16[80,128]{1,0:T(8,128)(2,1)S(1)} %get-tuple-element.19), channel_id=1, source_target_pairs={{0,200},{8,192},{16,216},{24,208},{32,232},{40,224},{48,248},{56,2... | collective-permute-start | bytes 61448 | tf_op jit(solution)/shard_map/ppermute | solution.py:27
  38.1 1.2 %collective-permute-start.13 = (bf16[80,128]{1,0:T(8,128)(2,1)S(1)}, bf16[80,128]{1,0:T(8,128)(2,1)S(1)}, u32[]{:S(2)}, u32[]{:S(2)}) collective-permute-start(bf16[80,128]{1,0:T(8,128)(2,1)S(1)} %get-tuple-element.20), channel_id=1, source_target_pairs={{0,64},{8,72},{16,80},{24,88},{32,96},{40,104},{48,112},{56,120},{... | collective-permute-start | bytes 61448 | tf_op jit(solution)/shard_map/ppermute | solution.py:27
  39.3 1.7 %fetch.3.refs_7_ = bf16[256,5120]{1,0:T(8,128)(2,1)S(1)} custom-call(bf16[640,5120]{1,0:T(8,128)(2,1)} %w_hbm.3), custom_call_target="tpu_custom_call" | custom-call | bytes 4194304 | tf_op jit(solution)/shard_map/fetch/pallas_call | solution.py:132
  41.1 1.8 %fetch.2.refs_6_ = bf16[256,5120]{1,0:T(8,128)(2,1)S(1)} custom-call(bf16[640,5120]{1,0:T(8,128)(2,1)} %w_hbm.3), custom_call_target="tpu_custom_call" | custom-call | bytes 4194304 | tf_op jit(solution)/shard_map/fetch/pallas_call | solution.py:132
  42.9 1.1 %project.1 = bf16[8,16,640]{2,1,0:T(8,128)(2,1)S(1)} custom-call(bf16[80,128]{1,0:T(8,128)(2,1)S(1)} %get-tuple-element.17.refs_0_, bf16[80,128]{1,0:T(8,128)(2,1)S(1)} %collective-permute-done.11.refs_1_, bf16[80,128]{1,0:T(8,128)(2,1)S(1)} %collective-permute-done.12.refs_2_, bf16[80,128]{1,0:T(8,128)(2,1)S(1)} %collective-permute-done.13.refs_3_, ...), custom_call_target="tpu_custom_call" | custom-call | tf_op jit(solution)/shard_map/project/pallas_call | solution.py:197
  43.9 11.7 %all_to_all.5 = bf16[8,16,640]{2,1,0:T(8,128)(2,1)S(1)} all-to-all(bf16[8,16,640]{2,1,0:T(8,128)(2,1)S(1)} %project.1), channel_id=1, replica_groups=mesh['seq'=32,'head'=8] {'head'}, dimensions={0} | all-to-all | bytes 327680 | tf_op jit(solution)/shard_map/all_to_all | solution.py:246
  55.7 0.6 %reduce_sum.12 = bf16[16,640]{1,0:T(8,128)(2,1)} reduce(bf16[8,16,640]{2,1,0:T(8,128)(2,1)S(1)} %all_to_all.5, bf16[]{:T(256)} %constant.2.clone.1), dimensions={0}, to_apply=%region_0.0 | reduce | flops 71680 | bytes 184322 | tf_op jit(solution)/shard_map/reduce_sum | solution.py:247
  (16 shorter events, 1.8 us)
Async XLA Ops:
  0.0 16.9 %collective-permute-start.3 = (bf16[2048,128]{1,0:T(8,128)(2,1)}, bf16[2048,128]{1,0:T(8,128)(2,1)S(1)}, u32[]{:S(2)}, u32[]{:S(2)}) collective-permute-start(bf16[2048,128]{1,0:T(8,128)(2,1)} %bitcast.5), channel_id=1, source_target_pairs={{0,8},{8,0},{16,24},{24,16},{32,40},{40,32},{48,56},{56,48},{64,72... | collective-permute-start | bytes 1572872 | tf_op jit(solution)/shard_map/ppermute | solution.py:218
  0.0 16.9 %collective-permute-start.4 = (bf16[2048,128]{1,0:T(8,128)(2,1)}, bf16[2048,128]{1,0:T(8,128)(2,1)S(1)}, u32[]{:S(2)}, u32[]{:S(2)}) collective-permute-start(bf16[2048,128]{1,0:T(8,128)(2,1)} %bitcast.7), channel_id=1, source_target_pairs={{0,8},{8,0},{16,24},{24,16},{32,40},{40,32},{48,56},{56,48},{64,72... | collective-permute-start | bytes 1572872 | tf_op jit(solution)/shard_map/ppermute | solution.py:219
  0.5 9.1 %collective-permute-start.2 = (bf16[80,128]{1,0:T(8,128)(2,1)}, bf16[80,128]{1,0:T(8,128)(2,1)S(1)}, u32[]{:S(2)}, u32[]{:S(2)}) collective-permute-start(bf16[80,128]{1,0:T(8,128)(2,1)} %bitcast.9), channel_id=1, source_target_pairs={{0,200},{8,192},{16,216},{24,208},{32,232},{40,224},{48,248},{56,2... | collective-permute-start | bytes 61448 | tf_op jit(solution)/shard_map/ppermute | solution.py:27
  5.5 7.3 %collective-permute-start.1 = (bf16[80,128]{1,0:T(8,128)(2,1)}, bf16[80,128]{1,0:T(8,128)(2,1)S(1)}, u32[]{:S(2)}, u32[]{:S(2)}) collective-permute-start(bf16[80,128]{1,0:T(8,128)(2,1)} %bitcast.10), channel_id=1, source_target_pairs={{0,136},{8,128},{16,152},{24,144},{32,168},{40,160},{48,184},{56,1... | collective-permute-start | bytes 61448 | tf_op jit(solution)/shard_map/ppermute | solution.py:27
  7.1 5.8 %collective-permute-start = (bf16[80,128]{1,0:T(8,128)(2,1)}, bf16[80,128]{1,0:T(8,128)(2,1)S(1)}, u32[]{:S(2)}, u32[]{:S(2)}) collective-permute-start(bf16[80,128]{1,0:T(8,128)(2,1)} %bitcast.11), channel_id=1, source_target_pairs={{0,64},{8,72},{16,80},{24,88},{32,96},{40,104},{48,112},{56,120},{... | collective-permute-start | bytes 61448 | tf_op jit(solution)/shard_map/ppermute | solution.py:27
  12.9 6.1 %collective-permute-start.5 = (bf16[4,80,128]{2,1,0:T(8,128)(2,1)S(1)}, bf16[4,80,128]{2,1,0:T(8,128)(2,1)S(1)}, u32[]{:S(2)}, u32[]{:S(2)}) collective-permute-start(bf16[4,80,128]{2,1,0:T(8,128)(2,1)S(1)} %join.1.q_ref), channel_id=1, source_target_pairs={{0,40},{8,32},{16,56},{24,48},{32,8},{40,0},{48,24},{56,16},{64,10... | collective-permute-start | bytes 245768 | tf_op jit(solution)/shard_map/ppermute | solution.py:27
  16.1 7.2 %collective-permute-start.9 = (bf16[4,80,128]{2,1,0:T(8,128)(2,1)S(1)}, bf16[4,80,128]{2,1,0:T(8,128)(2,1)S(1)}, u32[]{:S(2)}, u32[]{:S(2)}) collective-permute-start(bf16[4,80,128]{2,1,0:T(8,128)(2,1)S(1)} %join.1.q_ref), channel_id=1, source_target_pairs={{0,24},{8,16},{16,8},{24,0},{32,56},{40,48},{48,40},{56,32},{64,88... | collective-permute-start | bytes 245768 | tf_op jit(solution)/shard_map/ppermute | solution.py:27
  16.3 5.3 %collective-permute-start.7 = (bf16[4,80,128]{2,1,0:T(8,128)(2,1)S(1)}, bf16[4,80,128]{2,1,0:T(8,128)(2,1)S(1)}, u32[]{:S(2)}, u32[]{:S(2)}) collective-permute-start(bf16[4,80,128]{2,1,0:T(8,128)(2,1)S(1)} %join.1.q_ref), channel_id=1, source_target_pairs={{0,56},{8,48},{16,40},{24,32},{32,24},{40,16},{48,8},{56,0},{64,12... | collective-permute-start | bytes 245768 | tf_op jit(solution)/shard_map/ppermute | solution.py:27
  25.0 4.1 %collective-permute-start.10 = (bf16[4,80,128]{2,1,0:T(8,128)(2,1)S(1)}, bf16[4,80,128]{2,1,0:T(8,128)(2,1)S(1)}, u32[]{:S(2)}, u32[]{:S(2)}) collective-permute-start(bf16[4,80,128]{2,1,0:T(8,128)(2,1)S(1)} %read.7), channel_id=1, source_target_pairs={{0,24},{8,16},{16,8},{24,0},{32,56},{40,48},{48,40},{56,32},{64,88... | collective-permute-start | bytes 245768 | tf_op jit(solution)/shard_map/ppermute | solution.py:27
  26.1 6.0 %collective-permute-start.8 = (bf16[4,80,128]{2,1,0:T(8,128)(2,1)S(1)}, bf16[4,80,128]{2,1,0:T(8,128)(2,1)S(1)}, u32[]{:S(2)}, u32[]{:S(2)}) collective-permute-start(bf16[4,80,128]{2,1,0:T(8,128)(2,1)S(1)} %read.6.after_ref), channel_id=1, source_target_pairs={{0,56},{8,48},{16,40},{24,32},{32,24},{40,16},{48,8},{56,0},{64,12... | collective-permute-start | bytes 245768 | tf_op jit(solution)/shard_map/ppermute | solution.py:27
  27.6 5.4 %collective-permute-start.6 = (bf16[4,80,128]{2,1,0:T(8,128)(2,1)S(1)}, bf16[4,80,128]{2,1,0:T(8,128)(2,1)S(1)}, u32[]{:S(2)}, u32[]{:S(2)}) collective-permute-start(bf16[4,80,128]{2,1,0:T(8,128)(2,1)S(1)} %read.5.after_ref), channel_id=1, source_target_pairs={{0,40},{8,32},{16,56},{24,48},{32,8},{40,0},{48,24},{56,16},{64,10... | collective-permute-start | bytes 245768 | tf_op jit(solution)/shard_map/ppermute | solution.py:27
  33.0 9.8 %collective-permute-start.11 = (bf16[80,128]{1,0:T(8,128)(2,1)S(1)}, bf16[80,128]{1,0:T(8,128)(2,1)S(1)}, u32[]{:S(2)}, u32[]{:S(2)}) collective-permute-start(bf16[80,128]{1,0:T(8,128)(2,1)S(1)} %get-tuple-element.18), channel_id=1, source_target_pairs={{0,136},{8,128},{16,152},{24,144},{32,168},{40,160},{48,184},{56,1... | collective-permute-start | bytes 61448 | tf_op jit(solution)/shard_map/ppermute | solution.py:27
  36.7 6.2 %collective-permute-start.12 = (bf16[80,128]{1,0:T(8,128)(2,1)S(1)}, bf16[80,128]{1,0:T(8,128)(2,1)S(1)}, u32[]{:S(2)}, u32[]{:S(2)}) collective-permute-start(bf16[80,128]{1,0:T(8,128)(2,1)S(1)} %get-tuple-element.19), channel_id=1, source_target_pairs={{0,200},{8,192},{16,216},{24,208},{32,232},{40,224},{48,248},{56,2... | collective-permute-start | bytes 61448 | tf_op jit(solution)/shard_map/ppermute | solution.py:27
  38.1 4.8 %collective-permute-start.13 = (bf16[80,128]{1,0:T(8,128)(2,1)S(1)}, bf16[80,128]{1,0:T(8,128)(2,1)S(1)}, u32[]{:S(2)}, u32[]{:S(2)}) collective-permute-start(bf16[80,128]{1,0:T(8,128)(2,1)S(1)} %get-tuple-element.20), channel_id=1, source_target_pairs={{0,64},{8,72},{16,80},{24,88},{32,96},{40,104},{48,112},{56,120},{... | collective-permute-start | bytes 61448 | tf_op jit(solution)/shard_map/ppermute | solution.py:27

commit v4 on v3

--- a/solution.py
+++ b/solution.py
@@ -8,9 +8,11 @@
 from jax.sharding import PartitionSpec as P
 
 CONTRACT_LAST = (((1,), (1,)), ((), ()))
-KEY_TILE = 256
+KEY_TILE = 2048
+TURN_TILE = 256
 X_CHIPS, Z_BLOCKS, CORES = 4, 4, 2
 ORDER = (2, 3, 1)
+GROUPS = ((0,), (2,), (3, 1))
 
 
 def seq_index(z_block, x_chip, core):
@@ -39,34 +41,49 @@
     return pltpu.CompilerParams(vmem_limit_bytes=mib << 20)
 
 
-def stage_kernel(*refs):
-    count = len(refs) // 2
-    copies = []
-    for i in range(count):
-        source, target = refs[i], refs[count + i]
-        if source.shape != target.shape:
-            source = source.at[pl.ds(0, target.shape[0]), :]
-        copies.append(pltpu.make_async_copy(source, target, refs[-1].at[i]))
+def stage_kernel(
+    q_hbm, k_hbm, v_hbm, g_hbm, w_hbm, q_ref, k_ref, vt_ref, g_ref, w_ref, v_ref, sems
+):
+    routes = (
+        (v_hbm, v_ref),
+        (k_hbm, k_ref),
+        (q_hbm, q_ref),
+        (g_hbm, g_ref),
+        (w_hbm.at[pl.ds(0, w_ref.shape[0]), :], w_ref),
+    )
+    copies = [pltpu.make_async_copy(a, b, sems.at[i]) for i, (a, b) in enumerate(routes)]
     for copy in copies:
         copy.start()
-    for copy in copies:
+    copies[0].wait()
+    for start in range(0, v_ref.shape[0], TURN_TILE):
+        vt_ref[:, start : start + TURN_TILE] = v_ref[pl.ds(start, TURN_TILE), :].T
+    for copy in copies[1:]:
         copy.wait()
 
 
-def stage(*arrays, row_counts):
+def stage(rows, keys, values, gain, weight, weight_rows):
+    def like(array, *shape):
+        return jax.ShapeDtypeStruct(shape or array.shape, array.dtype)
+
     return pl.pallas_call(
         stage_kernel,
-        out_shape=tuple(
-            jax.ShapeDtypeStruct((count,) + a.shape[1:], a.dtype)
-            for a, count in zip(arrays, row_counts)
+        out_shape=(
+            like(rows),
+            like(keys),
+            like(values, *values.shape[::-1]),
+            like(gain),
+            like(weight, weight_rows, weight.shape[1]),
         ),
-        in_specs=[HBM] * len(arrays),
-        out_specs=(VMEM,) * len(arrays),
-        scratch_shapes=[pltpu.SemaphoreType.DMA((len(arrays),))],
-        compiler_params=params(4),
+        in_specs=[HBM] * 5,
+        out_specs=(VMEM,) * 5,
+        scratch_shapes=[
+            pltpu.VMEM(values.shape, values.dtype),
+            pltpu.SemaphoreType.DMA((5,)),
+        ],
+        compiler_params=params(6),
         cost_estimate=pl.CostEstimate(flops=0, bytes_accessed=4 << 20, transcendentals=0),
         name="stage",
-    )(*(in_hbm(a) for a in arrays))
+    )(*(in_hbm(a) for a in (rows, keys, values, gain, weight)))
 
 
 def join_kernel(*refs):
@@ -86,40 +103,45 @@
     )(*arrays)
 
 
-def read_rows(q_ref, pairs, o_ref):
-    chunks, count, width = q_ref.shape
-    rows = q_ref[...].reshape(chunks * count, width)
+def read_kernel(count, *refs):
+    q_refs, document, o_refs = refs[:count], refs[count:-count], refs[-count:]
+    slots, height, width = q_refs[0].shape
+    rows = jnp.concatenate([r[...].reshape(slots * height, width) for r in q_refs], axis=0)
     total = None
-    for k_ref, v_ref in pairs:
+    for k_ref, vt_ref in zip(document[::2], document[1::2]):
         for start in range(0, k_ref.shape[0], KEY_TILE):
-            tile = pl.ds(start, KEY_TILE)
             scores = lax.dot_general(
-                rows, k_ref[tile, :], CONTRACT_LAST, preferred_element_type=jnp.float32
+                k_ref[pl.ds(start, KEY_TILE), :],
+                rows,
+                CONTRACT_LAST,
+                preferred_element_type=jnp.float32,
             )
             weights = (scores * scores).astype(jnp.bfloat16)
-            term = jnp.dot(weights, v_ref[tile, :], preferred_element_type=jnp.float32)
+            term = jnp.dot(
+                vt_ref[:, start : start + KEY_TILE], weights, preferred_element_type=jnp.float32
+            )
             total = term if total is None else total + term
-    o_ref[...] = total.astype(o_ref.dtype).reshape(q_ref.shape)
-
-
-def read_kernel(q_ref, k0_ref, v0_ref, k1_ref, v1_ref, after_ref, o_ref):
-    read_rows(q_ref, ((k0_ref, v0_ref), (k1_ref, v1_ref)), o_ref)
-
-
-def read(rows, document, after):
-    tokens = sum(a.shape[0] for a in document) // 2
-    size = rows.shape[0] * rows.shape[1]
-    return pl.pallas_call(
-        read_kernel,
-        out_shape=jax.ShapeDtypeStruct(rows.shape, jnp.bfloat16),
-        in_specs=[VMEM] * 5 + [pl.BlockSpec(memory_space=pl.ANY)],
-        out_specs=VMEM,
-        compiler_params=params(16),
+    result = total.T.astype(o_refs[0].dtype)
+    for i, o_ref in enumerate(o_refs):
+        first = i * slots * height
+        o_ref[...] = result[first : first + slots * height, :].reshape(o_ref.shape)
+
+
+def read(chunks, document):
+    tokens = sum(a.shape[0] for a in document[::2])
+    size = len(chunks) * chunks[0].size
+    out = jax.ShapeDtypeStruct(chunks[0].shape, jnp.bfloat16)
+    return pl.pallas_call(
+        functools.partial(read_kernel, len(chunks)),
+        out_shape=(out,) * len(chunks),
+        in_specs=[VMEM] * (len(chunks) + len(document)),
+        out_specs=(VMEM,) * len(chunks),
+        compiler_params=params(32),
         cost_estimate=pl.CostEstimate(
-            flops=4 * size * tokens * rows.shape[2], bytes_accessed=4 << 20, transcendentals=0
+            flops=4 * size * tokens, bytes_accessed=4 << 20, transcendentals=0
         ),
         name="read",
-    )(rows, *document, after)
+    )(*chunks, *document)
 
 
 def fetch_kernel(first_row, w_hbm, w_ref, sem):
@@ -216,24 +238,20 @@
         from_z[steps] = exchange(own, steps, 0, steps >> 1)
     other_core = [(i, i ^ 1) for i in range(lax.axis_size("seq"))]
     near_keys = lax.ppermute(keys, "seq", other_core)
-    near_values = lax.ppermute(values, "seq", other_core)
-    staged_own, staged_keys, staged_values, gain, weight = stage(
-        own,
-        keys,
-        values,
-        out_gain,
-        out_weight,
-        row_counts=(heads * rows, tokens, tokens, heads, width),
+    staged_own, staged_keys, staged_turned, gain, weight = stage(
+        own, keys, values, out_gain, out_weight, width
     )
+    near_turned = lax.ppermute(staged_turned, "seq", other_core)
     column = join([staged_own, *(from_z[steps] for steps in range(1, Z_BLOCKS))])
-    document = (staged_keys, staged_values, near_keys, near_values)
+    document = (staged_keys, staged_turned, near_keys, near_turned)
     from_x = {}
     for steps in ORDER:
         from_x[steps] = exchange(column, 0, steps, 1)
-    part, parts = staged_own, []
-    for steps in (0, *ORDER):
-        part = read(from_x[steps] if steps else column, document, part)
-        parts.append(exchange(part, 0, steps, 1) if steps else part)
+    parts = []
+    for group in GROUPS:
+        results = read(tuple(from_x[steps] if steps else column for steps in group), document)
+        for steps, result in zip(group, results):
+            parts.append(exchange(result, 0, steps, 1) if steps else result)
     middle = width * (1 + (heads - 1) // 2)
     middle_weight = fetch(out_weight, width, middle - width)
     last_weight = fetch(out_weight, middle, heads * width - middle)

time: 57.4 us -> 60.3 us (1.051)
  the two profiles are of different devices: /device:TPU:32 before, /device:TPU:2 now
where the time goes in v4:
time: 60.3 us; the launch traced here: 60.1 us
  starting transfers between devices  25.3 us (42%)
  Pallas kernels  11.9 us (20%)
  blocking collectives  11.9 us (20%)
  waiting for transfers between devices  10.3 us (17%)
  other arithmetic  0.63 us (1%)
    ppermute x12, starting transfers between devices, exchange(): return lax.ppermute(rows, 'seq', pairs)  24.7 us
    all_to_all x1, blocking collectives, layer(): pieces = lax.all_to_all(projected, 'head', 0, 0, tiled=True)  11.9 us
    ppermute x12, waiting for transfers between devices, exchange(): return lax.ppermute(rows, 'seq', pairs)  10.3 us
    pallas_call x3, Pallas kernels, read(): pl.pallas_call(functools.partial(read_kernel, len(chunks)), out_shape=(ou...  5.55 us
    pallas_call x2, Pallas kernels, fetch(): pl.pallas_call(functools.partial(fetch_kernel, first_row), out_shape=jax....  3.5 us
    pallas_call x1, Pallas kernels, stage(): pl.pallas_call(stage_kernel, out_shape=(like(rows), like(keys), like(valu...  1.72 us
  transfers between devices with their start and end apart: 14, of which 5 were waited for; matrix products, arithmetic and copies ran while one was open for 0% of the time, Pallas kernels for 18%

profile of v4, /device:TPU:2, one launch (start us, length us, event | category | flops | bytes accessed | tf_op | source)
XLA Modules:
  0.0 60.1 jit_solution(13124529589004009246)
XLA Ops:
  0.0 1.7 %stage.1 = (bf16[80,128]{1,0:T(8,128)(2,1)S(1)}, bf16[2048,128]{1,0:T(8,128)(2,1)S(1)}, bf16[128,2048]{1,0:T(8,128)(2,1)S(1)}, f32[5,128]{1,0:T(8,128)S(1)}, bf16[128,5120]{1,0:T(8,128)(2,1)S(1)}) custom-call(bf16[80,128]{1,0:T(8,128)(2,1)} %bitcast.8, bf16[2048,128]{1,0:T(8,128)(2,1)} %bitcast.7, bf16[2048,128]{1,0:T(8,128)(2,1)} %bitcast.5, ...), custom_call_target="tpu_custom_call" | custom-call | bytes 4194304 | tf_op jit(solution)/shard_map/stage/pallas_call | solution.py:68
  2.3 6.0 %collective-permute-start.2 = (bf16[80,128]{1,0:T(8,128)(2,1)S(1)}, bf16[80,128]{1,0:T(8,128)(2,1)S(1)}, u32[]{:S(2)}, u32[]{:S(2)}) collective-permute-start(bf16[80,128]{1,0:T(8,128)(2,1)S(1)} %bitcast.9), channel_id=1, source_target_pairs={{0,200},{8,192},{16,216},{24,208},{32,232},{40,224},{48,248},{56,2... | collective-permute-start | bytes 61448 | tf_op jit(solution)/shard_map/ppermute | solution.py:29
  8.3 1.0 %collective-permute-start.1 = (bf16[80,128]{1,0:T(8,128)(2,1)S(1)}, bf16[80,128]{1,0:T(8,128)(2,1)S(1)}, u32[]{:S(2)}, u32[]{:S(2)}) collective-permute-start(bf16[80,128]{1,0:T(8,128)(2,1)S(1)} %bitcast.10), channel_id=1, source_target_pairs={{0,136},{8,128},{16,152},{24,144},{32,168},{40,160},{48,184},{56,1... | collective-permute-start | bytes 61448 | tf_op jit(solution)/shard_map/ppermute | solution.py:29
  9.3 1.5 %collective-permute-start = (bf16[80,128]{1,0:T(8,128)(2,1)S(1)}, bf16[80,128]{1,0:T(8,128)(2,1)S(1)}, u32[]{:S(2)}, u32[]{:S(2)}) collective-permute-start(bf16[80,128]{1,0:T(8,128)(2,1)S(1)} %bitcast.11), channel_id=1, source_target_pairs={{0,64},{8,72},{16,80},{24,88},{32,96},{40,104},{48,112},{56,120},{... | collective-permute-start | bytes 61448 | tf_op jit(solution)/shard_map/ppermute | solution.py:29
  10.8 4.9 %collective-permute-done.1.refs_2_ = bf16[80,128]{1,0:T(8,128)(2,1)S(1)} collective-permute-done((bf16[80,128]{1,0:T(8,128)(2,1)S(1)}, bf16[80,128]{1,0:T(8,128)(2,1)S(1)}, u32[]{:S(2)}, u32[]{:S(2)}) %collective-permute-start.1) | collective-permute-done | bytes 20512 | tf_op jit(solution)/shard_map/ppermute | solution.py:29
  16.1 2.1 %collective-permute-start.7 = (bf16[4,80,128]{2,1,0:T(8,128)(2,1)S(1)}, bf16[4,80,128]{2,1,0:T(8,128)(2,1)S(1)}, u32[]{:S(2)}, u32[]{:S(2)}) collective-permute-start(bf16[4,80,128]{2,1,0:T(8,128)(2,1)S(1)} %join.1.refs_0_), channel_id=1, source_target_pairs={{0,56},{8,48},{16,40},{24,32},{32,24},{40,16},{48,8},{56,0},{64,12... | collective-permute-start | bytes 245768 | tf_op jit(solution)/shard_map/ppermute | solution.py:29
  18.2 1.2 %collective-permute-start.5 = (bf16[4,80,128]{2,1,0:T(8,128)(2,1)S(1)}, bf16[4,80,128]{2,1,0:T(8,128)(2,1)S(1)}, u32[]{:S(2)}, u32[]{:S(2)}) collective-permute-start(bf16[4,80,128]{2,1,0:T(8,128)(2,1)S(1)} %join.1.refs_0_), channel_id=1, source_target_pairs={{0,40},{8,32},{16,56},{24,48},{32,8},{40,0},{48,24},{56,16},{64,10... | collective-permute-start | bytes 245768 | tf_op jit(solution)/shard_map/ppermute | solution.py:29
  19.4 0.8 %collective-permute-done.8.refs_1_ = bf16[4,80,128]{2,1,0:T(8,128)(2,1)S(1)} collective-permute-done((bf16[4,80,128]{2,1,0:T(8,128)(2,1)S(1)}, bf16[4,80,128]{2,1,0:T(8,128)(2,1)S(1)}, u32[]{:S(2)}, u32[]{:S(2)}) %collective-permute-start.8) | collective-permute-done | bytes 81952 | tf_op jit(solution)/shard_map/ppermute | solution.py:29
  20.2 0.7 %collective-permute-done.7.refs_0_ = bf16[4,80,128]{2,1,0:T(8,128)(2,1)S(1)} collective-permute-done((bf16[4,80,128]{2,1,0:T(8,128)(2,1)S(1)}, bf16[4,80,128]{2,1,0:T(8,128)(2,1)S(1)}, u32[]{:S(2)}, u32[]{:S(2)}) %collective-permute-start.7) | collective-permute-done | bytes 81952 | tf_op jit(solution)/shard_map/ppermute | solution.py:29
  20.8 2.4 %read.5 = (bf16[4,80,128]{2,1,0:T(8,128)(2,1)S(1)}, bf16[4,80,128]{2,1,0:T(8,128)(2,1)S(1)}) custom-call(bf16[4,80,128]{2,1,0:T(8,128)(2,1)S(1)} %collective-permute-done.7.refs_0_, bf16[4,80,128]{2,1,0:T(8,128)(2,1)S(1)} %collective-permute-done.8.refs_1_, bf16[2048,128]{1,0:T(8,128)(2,1)S(1)} %get-tuple-element.17.refs_1_.refs_2_, ...), custom_call_target="tpu_custom_call" | custom-call | flops 1342177280 | bytes 4194304 | tf_op jit(solution)/shard_map/read/pallas_call | solution.py:134
  23.2 3.5 %collective-permute-start.9 = (bf16[4,80,128]{2,1,0:T(8,128)(2,1)S(1)}, bf16[4,80,128]{2,1,0:T(8,128)(2,1)S(1)}, u32[]{:S(2)}, u32[]{:S(2)}) collective-permute-start(bf16[4,80,128]{2,1,0:T(8,128)(2,1)S(1)} %get-tuple-element.19), channel_id=1, source_target_pairs={{0,56},{8,48},{16,40},{24,32},{32,24},{40,16},{48,8},{56,0},{64,12... | collective-permute-start | bytes 245768 | tf_op jit(solution)/shard_map/ppermute | solution.py:29
  26.7 0.7 %collective-permute-start.10 = (bf16[4,80,128]{2,1,0:T(8,128)(2,1)S(1)}, bf16[4,80,128]{2,1,0:T(8,128)(2,1)S(1)}, u32[]{:S(2)}, u32[]{:S(2)}) collective-permute-start(bf16[4,80,128]{2,1,0:T(8,128)(2,1)S(1)} %get-tuple-element.20), channel_id=1, source_target_pairs={{0,24},{8,16},{16,8},{24,0},{32,56},{40,48},{48,40},{56,32},{64,88... | collective-permute-start | bytes 245768 | tf_op jit(solution)/shard_map/ppermute | solution.py:29
  27.4 1.6 %read.4 = bf16[4,80,128]{2,1,0:T(8,128)(2,1)S(1)} custom-call(bf16[4,80,128]{2,1,0:T(8,128)(2,1)S(1)} %collective-permute-done.5.refs_0_, bf16[2048,128]{1,0:T(8,128)(2,1)S(1)} %get-tuple-element.17.refs_1_.refs_2_, bf16[128,2048]{1,0:T(8,128)(2,1)S(1)} %get-tuple-element.18.refs_2_.refs_3_, bf16[2048,128]{1,0:T(8,128)(2,1)S(1)} %collective-permute-done.3.refs_3_.refs_4_, ...), custom_call_target="tpu_custom_call" | custom-call | flops 671088640 | bytes 4194304 | tf_op jit(solution)/shard_map/read/pallas_call | solution.py:134
  29.0 1.0 %collective-permute-start.6 = (bf16[4,80,128]{2,1,0:T(8,128)(2,1)S(1)}, bf16[4,80,128]{2,1,0:T(8,128)(2,1)S(1)}, u32[]{:S(2)}, u32[]{:S(2)}) collective-permute-start(bf16[4,80,128]{2,1,0:T(8,128)(2,1)S(1)} %read.4), channel_id=1, source_target_pairs={{0,40},{8,32},{16,56},{24,48},{32,8},{40,0},{48,24},{56,16},{64,10... | collective-permute-start | bytes 245768 | tf_op jit(solution)/shard_map/ppermute | solution.py:29
  30.0 1.6 %read.3.refs_0_ = bf16[4,80,128]{2,1,0:T(8,128)(2,1)S(1)} custom-call(bf16[4,80,128]{2,1,0:T(8,128)(2,1)S(1)} %join.1.refs_0_, bf16[2048,128]{1,0:T(8,128)(2,1)S(1)} %get-tuple-element.17.refs_1_.refs_2_, bf16[128,2048]{1,0:T(8,128)(2,1)S(1)} %get-tuple-element.18.refs_2_.refs_3_, bf16[2048,128]{1,0:T(8,128)(2,1)S(1)} %collective-permute-done.3.refs_3_.refs_4_, ...), custom_call_target="tpu_custom_call" | custom-call | flops 671088640 | bytes 4194304 | tf_op jit(solution)/shard_map/read/pallas_call | solution.py:134
  31.6 2.9 %collective-permute-done.6.refs_1_ = bf16[4,80,128]{2,1,0:T(8,128)(2,1)S(1)} collective-permute-done((bf16[4,80,128]{2,1,0:T(8,128)(2,1)S(1)}, bf16[4,80,128]{2,1,0:T(8,128)(2,1)S(1)}, u32[]{:S(2)}, u32[]{:S(2)}) %collective-permute-start.6) | collective-permute-done | bytes 81952 | tf_op jit(solution)/shard_map/ppermute | solution.py:29
  34.5 4.6 %collective-permute-start.11 = (bf16[80,128]{1,0:T(8,128)(2,1)S(1)}, bf16[80,128]{1,0:T(8,128)(2,1)S(1)}, u32[]{:S(2)}, u32[]{:S(2)}) collective-permute-start(bf16[80,128]{1,0:T(8,128)(2,1)S(1)} %get-tuple-element.22), channel_id=1, source_target_pairs={{0,136},{8,128},{16,152},{24,144},{32,168},{40,160},{48,184},{56,1... | collective-permute-start | bytes 61448 | tf_op jit(solution)/shard_map/ppermute | solution.py:29
  39.1 2.8 %collective-permute-start.12 = (bf16[80,128]{1,0:T(8,128)(2,1)S(1)}, bf16[80,128]{1,0:T(8,128)(2,1)S(1)}, u32[]{:S(2)}, u32[]{:S(2)}) collective-permute-start(bf16[80,128]{1,0:T(8,128)(2,1)S(1)} %get-tuple-element.23), channel_id=1, source_target_pairs={{0,200},{8,192},{16,216},{24,208},{32,232},{40,224},{48,248},{56,2... | collective-permute-start | bytes 61448 | tf_op jit(solution)/shard_map/ppermute | solution.py:29
  41.8 1.7 %fetch.3.refs_7_ = bf16[256,5120]{1,0:T(8,128)(2,1)S(1)} custom-call(bf16[640,5120]{1,0:T(8,128)(2,1)} %w_hbm.5), custom_call_target="tpu_custom_call" | custom-call | bytes 4194304 | tf_op jit(solution)/shard_map/fetch/pallas_call | solution.py:154
  43.6 1.8 %fetch.2.refs_6_ = bf16[256,5120]{1,0:T(8,128)(2,1)S(1)} custom-call(bf16[640,5120]{1,0:T(8,128)(2,1)} %w_hbm.5), custom_call_target="tpu_custom_call" | custom-call | bytes 4194304 | tf_op jit(solution)/shard_map/fetch/pallas_call | solution.py:154
  45.4 1.1 %collective-permute-done.13.refs_3_ = bf16[80,128]{1,0:T(8,128)(2,1)S(1)} collective-permute-done((bf16[80,128]{1,0:T(8,128)(2,1)S(1)}, bf16[80,128]{1,0:T(8,128)(2,1)S(1)}, u32[]{:S(2)}, u32[]{:S(2)}) %collective-permute-start.13) | collective-permute-done | bytes 20512 | tf_op jit(solution)/shard_map/ppermute | solution.py:29
  46.5 1.1 %project.1 = bf16[8,16,640]{2,1,0:T(8,128)(2,1)S(1)} custom-call(bf16[80,128]{1,0:T(8,128)(2,1)S(1)} %get-tuple-element.21.refs_0_, bf16[80,128]{1,0:T(8,128)(2,1)S(1)} %collective-permute-done.11.refs_1_, bf16[80,128]{1,0:T(8,128)(2,1)S(1)} %collective-permute-done.12.refs_2_, bf16[80,128]{1,0:T(8,128)(2,1)S(1)} %collective-permute-done.13.refs_3_, ...), custom_call_target="tpu_custom_call" | custom-call | tf_op jit(solution)/shard_map/project/pallas_call | solution.py:219
  47.6 11.9 %all_to_all.5 = bf16[8,16,640]{2,1,0:T(8,128)(2,1)S(1)} all-to-all(bf16[8,16,640]{2,1,0:T(8,128)(2,1)S(1)} %project.1), channel_id=1, replica_groups=mesh['seq'=32,'head'=8] {'head'}, dimensions={0} | all-to-all | bytes 327680 | tf_op jit(solution)/shard_map/all_to_all | solution.py:264
  59.5 0.6 %reduce_sum.12 = bf16[16,640]{1,0:T(8,128)(2,1)} reduce(bf16[8,16,640]{2,1,0:T(8,128)(2,1)S(1)} %all_to_all.5, bf16[]{:T(256)} %constant.2.clone.1), dimensions={0}, to_apply=%region_0.0 | reduce | flops 71680 | bytes 184322 | tf_op jit(solution)/shard_map/reduce_sum | solution.py:265
  (17 shorter events, 1.1 us)
Async XLA Ops:
  0.0 20.8 %collective-permute-start.3 = (bf16[2048,128]{1,0:T(8,128)(2,1)}, bf16[2048,128]{1,0:T(8,128)(2,1)S(1)}, u32[]{:S(2)}, u32[]{:S(2)}) collective-permute-start(bf16[2048,128]{1,0:T(8,128)(2,1)} %bitcast.6), channel_id=1, source_target_pairs={{0,8},{8,0},{16,24},{24,16},{32,40},{40,32},{48,56},{56,48},{64,72... | collective-permute-start | bytes 1572872 | tf_op jit(solution)/shard_map/ppermute | solution.py:240
  0.0 2.3 %copy-start = (bf16[16,5,128]{2,0,1:T(8,128)(2,1)S(1)}, bf16[16,5,128]{2,0,1:T(8,128)(2,1)}, u32[]{:S(2)}) copy-start(bf16[16,5,128]{2,0,1:T(8,128)(2,1)} %param.5) | copy-start | bytes 61444
  1.7 19.1 %collective-permute-start.4 = (bf16[128,2048]{1,0:T(8,128)(2,1)S(1)}, bf16[128,2048]{1,0:T(8,128)(2,1)S(1)}, u32[]{:S(2)}, u32[]{:S(2)}) collective-permute-start(bf16[128,2048]{1,0:T(8,128)(2,1)S(1)} %get-tuple-element.18.refs_2_.refs_3_), channel_id=1, source_target_pairs={{0,8},{8,0},{16,24},{24,16},{32,40},{40,32},{48,56},{56,48},{64,72... | collective-permute-start | bytes 1572872 | tf_op jit(solution)/shard_map/ppermute | solution.py:244
  2.3 8.5 %collective-permute-start.2 = (bf16[80,128]{1,0:T(8,128)(2,1)S(1)}, bf16[80,128]{1,0:T(8,128)(2,1)S(1)}, u32[]{:S(2)}, u32[]{:S(2)}) collective-permute-start(bf16[80,128]{1,0:T(8,128)(2,1)S(1)} %bitcast.9), channel_id=1, source_target_pairs={{0,200},{8,192},{16,216},{24,208},{32,232},{40,224},{48,248},{56,2... | collective-permute-start | bytes 61448 | tf_op jit(solution)/shard_map/ppermute | solution.py:29
  8.3 7.3 %collective-permute-start.1 = (bf16[80,128]{1,0:T(8,128)(2,1)S(1)}, bf16[80,128]{1,0:T(8,128)(2,1)S(1)}, u32[]{:S(2)}, u32[]{:S(2)}) collective-permute-start(bf16[80,128]{1,0:T(8,128)(2,1)S(1)} %bitcast.10), channel_id=1, source_target_pairs={{0,136},{8,128},{16,152},{24,144},{32,168},{40,160},{48,184},{56,1... | collective-permute-start | bytes 61448 | tf_op jit(solution)/shard_map/ppermute | solution.py:29
  9.3 6.3 %collective-permute-start = (bf16[80,128]{1,0:T(8,128)(2,1)S(1)}, bf16[80,128]{1,0:T(8,128)(2,1)S(1)}, u32[]{:S(2)}, u32[]{:S(2)}) collective-permute-start(bf16[80,128]{1,0:T(8,128)(2,1)S(1)} %bitcast.11), channel_id=1, source_target_pairs={{0,64},{8,72},{16,80},{24,88},{32,96},{40,104},{48,112},{56,120},{... | collective-permute-start | bytes 61448 | tf_op jit(solution)/shard_map/ppermute | solution.py:29
  15.7 4.5 %collective-permute-start.8 = (bf16[4,80,128]{2,1,0:T(8,128)(2,1)S(1)}, bf16[4,80,128]{2,1,0:T(8,128)(2,1)S(1)}, u32[]{:S(2)}, u32[]{:S(2)}) collective-permute-start(bf16[4,80,128]{2,1,0:T(8,128)(2,1)S(1)} %join.1.refs_0_), channel_id=1, source_target_pairs={{0,24},{8,16},{16,8},{24,0},{32,56},{40,48},{48,40},{56,32},{64,88... | collective-permute-start | bytes 245768 | tf_op jit(solution)/shard_map/ppermute | solution.py:29
  16.1 4.7 %collective-permute-start.7 = (bf16[4,80,128]{2,1,0:T(8,128)(2,1)S(1)}, bf16[4,80,128]{2,1,0:T(8,128)(2,1)S(1)}, u32[]{:S(2)}, u32[]{:S(2)}) collective-permute-start(bf16[4,80,128]{2,1,0:T(8,128)(2,1)S(1)} %join.1.refs_0_), channel_id=1, source_target_pairs={{0,56},{8,48},{16,40},{24,32},{32,24},{40,16},{48,8},{56,0},{64,12... | collective-permute-start | bytes 245768 | tf_op jit(solution)/shard_map/ppermute | solution.py:29
  18.2 9.2 %collective-permute-start.5 = (bf16[4,80,128]{2,1,0:T(8,128)(2,1)S(1)}, bf16[4,80,128]{2,1,0:T(8,128)(2,1)S(1)}, u32[]{:S(2)}, u32[]{:S(2)}) collective-permute-start(bf16[4,80,128]{2,1,0:T(8,128)(2,1)S(1)} %join.1.refs_0_), channel_id=1, source_target_pairs={{0,40},{8,32},{16,56},{24,48},{32,8},{40,0},{48,24},{56,16},{64,10... | collective-permute-start | bytes 245768 | tf_op jit(solution)/shard_map/ppermute | solution.py:29
  23.2 8.3 %collective-permute-start.9 = (bf16[4,80,128]{2,1,0:T(8,128)(2,1)S(1)}, bf16[4,80,128]{2,1,0:T(8,128)(2,1)S(1)}, u32[]{:S(2)}, u32[]{:S(2)}) collective-permute-start(bf16[4,80,128]{2,1,0:T(8,128)(2,1)S(1)} %get-tuple-element.19), channel_id=1, source_target_pairs={{0,56},{8,48},{16,40},{24,32},{32,24},{40,16},{48,8},{56,0},{64,12... | collective-permute-start | bytes 245768 | tf_op jit(solution)/shard_map/ppermute | solution.py:29
  26.7 4.8 %collective-permute-start.10 = (bf16[4,80,128]{2,1,0:T(8,128)(2,1)S(1)}, bf16[4,80,128]{2,1,0:T(8,128)(2,1)S(1)}, u32[]{:S(2)}, u32[]{:S(2)}) collective-permute-start(bf16[4,80,128]{2,1,0:T(8,128)(2,1)S(1)} %get-tuple-element.20), channel_id=1, source_target_pairs={{0,24},{8,16},{16,8},{24,0},{32,56},{40,48},{48,40},{56,32},{64,88... | collective-permute-start | bytes 245768 | tf_op jit(solution)/shard_map/ppermute | solution.py:29
  29.0 5.5 %collective-permute-start.6 = (bf16[4,80,128]{2,1,0:T(8,128)(2,1)S(1)}, bf16[4,80,128]{2,1,0:T(8,128)(2,1)S(1)}, u32[]{:S(2)}, u32[]{:S(2)}) collective-permute-start(bf16[4,80,128]{2,1,0:T(8,128)(2,1)S(1)} %read.4), channel_id=1, source_target_pairs={{0,40},{8,32},{16,56},{24,48},{32,8},{40,0},{48,24},{56,16},{64,10... | collective-permute-start | bytes 245768 | tf_op jit(solution)/shard_map/ppermute | solution.py:29
  34.5 10.9 %collective-permute-start.11 = (bf16[80,128]{1,0:T(8,128)(2,1)S(1)}, bf16[80,128]{1,0:T(8,128)(2,1)S(1)}, u32[]{:S(2)}, u32[]{:S(2)}) collective-permute-start(bf16[80,128]{1,0:T(8,128)(2,1)S(1)} %get-tuple-element.22), channel_id=1, source_target_pairs={{0,136},{8,128},{16,152},{24,144},{32,168},{40,160},{48,184},{56,1... | collective-permute-start | bytes 61448 | tf_op jit(solution)/shard_map/ppermute | solution.py:29
  39.1 6.3 %collective-permute-start.12 = (bf16[80,128]{1,0:T(8,128)(2,1)S(1)}, bf16[80,128]{1,0:T(8,128)(2,1)S(1)}, u32[]{:S(2)}, u32[]{:S(2)}) collective-permute-start(bf16[80,128]{1,0:T(8,128)(2,1)S(1)} %get-tuple-element.23), channel_id=1, source_target_pairs={{0,200},{8,192},{16,216},{24,208},{32,232},{40,224},{48,248},{56,2... | collective-permute-start | bytes 61448 | tf_op jit(solution)/shard_map/ppermute | solution.py:29
  41.8 4.7 %collective-permute-start.13 = (bf16[80,128]{1,0:T(8,128)(2,1)S(1)}, bf16[80,128]{1,0:T(8,128)(2,1)S(1)}, u32[]{:S(2)}, u32[]{:S(2)}) collective-permute-start(bf16[80,128]{1,0:T(8,128)(2,1)S(1)} %get-tuple-element.24), channel_id=1, source_target_pairs={{0,64},{8,72},{16,80},{24,88},{32,96},{40,104},{48,112},{56,120},{... | collective-permute-start | bytes 61448 | tf_op jit(solution)/shard_map/ppermute | solution.py:29

commit v5 on v4

--- a/solution.py
+++ b/solution.py
@@ -13,6 +13,8 @@
 X_CHIPS, Z_BLOCKS, CORES = 4, 4, 2
 ORDER = (2, 3, 1)
 GROUPS = ((0,), (2,), (3, 1))
+Z_FLIPS = (0, 0, 1, 1)
+X_FLIPS = (0, 1, 1, 0)
 
 
 def seq_index(z_block, x_chip, core):
@@ -235,7 +237,7 @@
     own = jnp.transpose(queries, (1, 0, 2)).reshape(heads * rows, width)
     from_z = {}
     for steps in ORDER:
-        from_z[steps] = exchange(own, steps, 0, steps >> 1)
+        from_z[steps] = exchange(own, steps, 0, Z_FLIPS[steps])
     other_core = [(i, i ^ 1) for i in range(lax.axis_size("seq"))]
     near_keys = lax.ppermute(keys, "seq", other_core)
     staged_own, staged_keys, staged_turned, gain, weight = stage(
@@ -246,12 +248,12 @@
     document = (staged_keys, staged_turned, near_keys, near_turned)
     from_x = {}
     for steps in ORDER:
-        from_x[steps] = exchange(column, 0, steps, 1)
+        from_x[steps] = exchange(column, 0, steps, X_FLIPS[steps])
     parts = []
     for group in GROUPS:
         results = read(tuple(from_x[steps] if steps else column for steps in group), document)
         for steps, result in zip(group, results):
-            parts.append(exchange(result, 0, steps, 1) if steps else result)
+            parts.append(exchange(result, 0, steps, X_FLIPS[steps]) if steps else result)
     middle = width * (1 + (heads - 1) // 2)
     middle_weight = fetch(out_weight, width, middle - width)
     last_weight = fetch(out_weight, middle, heads * width - middle)
@@ -259,7 +261,7 @@
     slots = add(parts)
     parts = [slots[0]]
     for steps in ORDER:
-        parts.append(exchange(slots[steps], steps, 0, steps >> 1))
+        parts.append(exchange(slots[steps], steps, 0, Z_FLIPS[steps]))
     projected = project(parts, gain, weights, head_groups)
     pieces = lax.all_to_all(projected, "head", 0, 0, tiled=True)
     return jnp.sum(pieces.astype(jnp.float32), axis=0).astype(jnp.bfloat16)

time: 60.3 us -> 59.2 us (0.982)
  the two profiles are of different devices: /device:TPU:2 before, /device:TPU:32 now
where the time goes in v5:
time: 59.2 us; the launch traced here: 58.5 us
  starting transfers between devices  23.3 us (39%)
  blocking collectives  12.3 us (21%)
  Pallas kernels  11.9 us (20%)
  waiting for transfers between devices  10.3 us (17%)
  other arithmetic  0.63 us (1%)
    ppermute x12, starting transfers between devices, exchange(): return lax.ppermute(rows, 'seq', pairs)  22.7 us
    all_to_all x1, blocking collectives, layer(): pieces = lax.all_to_all(projected, 'head', 0, 0, tiled=True)  12.3 us
    ppermute x12, waiting for transfers between devices, exchange(): return lax.ppermute(rows, 'seq', pairs)  10.2 us
    pallas_call x3, Pallas kernels, read(): pl.pallas_call(functools.partial(read_kernel, len(chunks)), out_shape=(ou...  5.55 us
    pallas_call x2, Pallas kernels, fetch(): pl.pallas_call(functools.partial(fetch_kernel, first_row), out_shape=jax....  3.5 us
    pallas_call x1, Pallas kernels, stage(): pl.pallas_call(stage_kernel, out_shape=(like(rows), like(keys), like(valu...  1.72 us
  transfers between devices with their start and end apart: 14, of which 5 were waited for; matrix products, arithmetic and copies ran while one was open for 0% of the time, Pallas kernels for 18%

profile of v5, /device:TPU:32, one launch (start us, length us, event | category | flops | bytes accessed | tf_op | source)
XLA Modules:
  0.0 58.5 jit_solution(9963149768287307080)
XLA Ops:
  0.0 1.7 %stage.1 = (bf16[80,128]{1,0:T(8,128)(2,1)S(1)}, bf16[2048,128]{1,0:T(8,128)(2,1)S(1)}, bf16[128,2048]{1,0:T(8,128)(2,1)S(1)}, f32[5,128]{1,0:T(8,128)S(1)}, bf16[128,5120]{1,0:T(8,128)(2,1)S(1)}) custom-call(bf16[80,128]{1,0:T(8,128)(2,1)} %bitcast.8, bf16[2048,128]{1,0:T(8,128)(2,1)} %bitcast.7, bf16[2048,128]{1,0:T(8,128)(2,1)} %bitcast.5, ...), custom_call_target="tpu_custom_call" | custom-call | bytes 4194304 | tf_op jit(solution)/shard_map/stage/pallas_call | solution.py:70
  1.7 0.6 %collective-permute-start.4 = (bf16[128,2048]{1,0:T(8,128)(2,1)S(1)}, bf16[128,2048]{1,0:T(8,128)(2,1)S(1)}, u32[]{:S(2)}, u32[]{:S(2)}) collective-permute-start(bf16[128,2048]{1,0:T(8,128)(2,1)S(1)} %get-tuple-element.18.refs_2_.refs_3_), channel_id=1, source_target_pairs={{0,8},{8,0},{16,24},{24,16},{32,40},{40,32},{48,56},{56,48},{64,72... | collective-permute-start | bytes 1572872 | tf_op jit(solution)/shard_map/ppermute | solution.py:246
  2.3 5.1 %collective-permute-start.2 = (bf16[80,128]{1,0:T(8,128)(2,1)S(1)}, bf16[80,128]{1,0:T(8,128)(2,1)S(1)}, u32[]{:S(2)}, u32[]{:S(2)}) collective-permute-start(bf16[80,128]{1,0:T(8,128)(2,1)S(1)} %bitcast.9), channel_id=1, source_target_pairs={{0,200},{8,192},{16,216},{24,208},{32,232},{40,224},{48,248},{56,2... | collective-permute-start | bytes 61448 | tf_op jit(solution)/shard_map/ppermute | solution.py:31
  7.4 1.4 %collective-permute-start.1 = (bf16[80,128]{1,0:T(8,128)(2,1)S(1)}, bf16[80,128]{1,0:T(8,128)(2,1)S(1)}, u32[]{:S(2)}, u32[]{:S(2)}) collective-permute-start(bf16[80,128]{1,0:T(8,128)(2,1)S(1)} %bitcast.10), channel_id=1, source_target_pairs={{0,136},{8,128},{16,152},{24,144},{32,168},{40,160},{48,184},{56,1... | collective-permute-start | bytes 61448 | tf_op jit(solution)/shard_map/ppermute | solution.py:31
  8.9 1.0 %collective-permute-start = (bf16[80,128]{1,0:T(8,128)(2,1)S(1)}, bf16[80,128]{1,0:T(8,128)(2,1)S(1)}, u32[]{:S(2)}, u32[]{:S(2)}) collective-permute-start(bf16[80,128]{1,0:T(8,128)(2,1)S(1)} %bitcast.11), channel_id=1, source_target_pairs={{0,64},{8,72},{16,80},{24,88},{32,96},{40,104},{48,112},{56,120},{... | collective-permute-start | bytes 61448 | tf_op jit(solution)/shard_map/ppermute | solution.py:31
  9.9 4.7 %collective-permute-done.1.refs_2_ = bf16[80,128]{1,0:T(8,128)(2,1)S(1)} collective-permute-done((bf16[80,128]{1,0:T(8,128)(2,1)S(1)}, bf16[80,128]{1,0:T(8,128)(2,1)S(1)}, u32[]{:S(2)}, u32[]{:S(2)}) %collective-permute-start.1) | collective-permute-done | bytes 20512 | tf_op jit(solution)/shard_map/ppermute | solution.py:31
  14.6 1.6 %collective-permute-start.8 = (bf16[4,80,128]{2,1,0:T(8,128)(2,1)S(1)}, bf16[4,80,128]{2,1,0:T(8,128)(2,1)S(1)}, u32[]{:S(2)}, u32[]{:S(2)}) collective-permute-start(bf16[4,80,128]{2,1,0:T(8,128)(2,1)S(1)} %join.1.refs_0_), channel_id=1, source_target_pairs={{0,24},{8,16},{16,8},{24,0},{32,56},{40,48},{48,40},{56,32},{64,88... | collective-permute-start | bytes 245768 | tf_op jit(solution)/shard_map/ppermute | solution.py:31
  16.2 2.1 %collective-permute-start.7 = (bf16[4,80,128]{2,1,0:T(8,128)(2,1)S(1)}, bf16[4,80,128]{2,1,0:T(8,128)(2,1)S(1)}, u32[]{:S(2)}, u32[]{:S(2)}) collective-permute-start(bf16[4,80,128]{2,1,0:T(8,128)(2,1)S(1)} %join.1.refs_0_), channel_id=1, source_target_pairs={{0,48},{8,56},{16,32},{24,40},{32,16},{40,24},{48,0},{56,8},{64,11... | collective-permute-start | bytes 245768 | tf_op jit(solution)/shard_map/ppermute | solution.py:31
  18.3 0.3 collective-permute-start.5
  18.8 3.0 %collective-permute-done.7.refs_0_ = bf16[4,80,128]{2,1,0:T(8,128)(2,1)S(1)} collective-permute-done((bf16[4,80,128]{2,1,0:T(8,128)(2,1)S(1)}, bf16[4,80,128]{2,1,0:T(8,128)(2,1)S(1)}, u32[]{:S(2)}, u32[]{:S(2)}) %collective-permute-start.7) | collective-permute-done | bytes 81952 | tf_op jit(solution)/shard_map/ppermute | solution.py:31
  21.8 2.4 %read.5 = (bf16[4,80,128]{2,1,0:T(8,128)(2,1)S(1)}, bf16[4,80,128]{2,1,0:T(8,128)(2,1)S(1)}) custom-call(bf16[4,80,128]{2,1,0:T(8,128)(2,1)S(1)} %collective-permute-done.7.refs_0_, bf16[4,80,128]{2,1,0:T(8,128)(2,1)S(1)} %collective-permute-done.8.refs_1_, bf16[2048,128]{1,0:T(8,128)(2,1)S(1)} %get-tuple-element.17.refs_1_.refs_2_, ...), custom_call_target="tpu_custom_call" | custom-call | flops 1342177280 | bytes 4194304 | tf_op jit(solution)/shard_map/read/pallas_call | solution.py:136
  24.2 2.2 %collective-permute-start.9 = (bf16[4,80,128]{2,1,0:T(8,128)(2,1)S(1)}, bf16[4,80,128]{2,1,0:T(8,128)(2,1)S(1)}, u32[]{:S(2)}, u32[]{:S(2)}) collective-permute-start(bf16[4,80,128]{2,1,0:T(8,128)(2,1)S(1)} %get-tuple-element.19), channel_id=1, source_target_pairs={{0,48},{8,56},{16,32},{24,40},{32,16},{40,24},{48,0},{56,8},{64,11... | collective-permute-start | bytes 245768 | tf_op jit(solution)/shard_map/ppermute | solution.py:31
  26.5 1.6 %read.4 = bf16[4,80,128]{2,1,0:T(8,128)(2,1)S(1)} custom-call(bf16[4,80,128]{2,1,0:T(8,128)(2,1)S(1)} %collective-permute-done.5.refs_0_, bf16[2048,128]{1,0:T(8,128)(2,1)S(1)} %get-tuple-element.17.refs_1_.refs_2_, bf16[128,2048]{1,0:T(8,128)(2,1)S(1)} %get-tuple-element.18.refs_2_.refs_3_, bf16[2048,128]{1,0:T(8,128)(2,1)S(1)} %collective-permute-done.3.refs_3_.refs_4_, ...), custom_call_target="tpu_custom_call" | custom-call | flops 671088640 | bytes 4194304 | tf_op jit(solution)/shard_map/read/pallas_call | solution.py:136
  28.0 2.4 %collective-permute-start.6 = (bf16[4,80,128]{2,1,0:T(8,128)(2,1)S(1)}, bf16[4,80,128]{2,1,0:T(8,128)(2,1)S(1)}, u32[]{:S(2)}, u32[]{:S(2)}) collective-permute-start(bf16[4,80,128]{2,1,0:T(8,128)(2,1)S(1)} %read.4), channel_id=1, source_target_pairs={{0,40},{8,32},{16,56},{24,48},{32,8},{40,0},{48,24},{56,16},{64,10... | collective-permute-start | bytes 245768 | tf_op jit(solution)/shard_map/ppermute | solution.py:31
  30.4 1.6 %read.3.refs_0_ = bf16[4,80,128]{2,1,0:T(8,128)(2,1)S(1)} custom-call(bf16[4,80,128]{2,1,0:T(8,128)(2,1)S(1)} %join.1.refs_0_, bf16[2048,128]{1,0:T(8,128)(2,1)S(1)} %get-tuple-element.17.refs_1_.refs_2_, bf16[128,2048]{1,0:T(8,128)(2,1)S(1)} %get-tuple-element.18.refs_2_.refs_3_, bf16[2048,128]{1,0:T(8,128)(2,1)S(1)} %collective-permute-done.3.refs_3_.refs_4_, ...), custom_call_target="tpu_custom_call" | custom-call | flops 671088640 | bytes 4194304 | tf_op jit(solution)/shard_map/read/pallas_call | solution.py:136
  32.0 2.0 %collective-permute-done.6.refs_1_ = bf16[4,80,128]{2,1,0:T(8,128)(2,1)S(1)} collective-permute-done((bf16[4,80,128]{2,1,0:T(8,128)(2,1)S(1)}, bf16[4,80,128]{2,1,0:T(8,128)(2,1)S(1)}, u32[]{:S(2)}, u32[]{:S(2)}) %collective-permute-start.6) | collective-permute-done | bytes 81952 | tf_op jit(solution)/shard_map/ppermute | solution.py:31
  34.1 5.1 %collective-permute-start.11 = (bf16[80,128]{1,0:T(8,128)(2,1)S(1)}, bf16[80,128]{1,0:T(8,128)(2,1)S(1)}, u32[]{:S(2)}, u32[]{:S(2)}) collective-permute-start(bf16[80,128]{1,0:T(8,128)(2,1)S(1)} %get-tuple-element.22), channel_id=1, source_target_pairs={{0,136},{8,128},{16,152},{24,144},{32,168},{40,160},{48,184},{56,1... | collective-permute-start | bytes 61448 | tf_op jit(solution)/shard_map/ppermute | solution.py:31
  39.2 1.4 %collective-permute-start.13 = (bf16[80,128]{1,0:T(8,128)(2,1)S(1)}, bf16[80,128]{1,0:T(8,128)(2,1)S(1)}, u32[]{:S(2)}, u32[]{:S(2)}) collective-permute-start(bf16[80,128]{1,0:T(8,128)(2,1)S(1)} %get-tuple-element.24), channel_id=1, source_target_pairs={{0,64},{8,72},{16,80},{24,88},{32,96},{40,104},{48,112},{56,120},{... | collective-permute-start | bytes 61448 | tf_op jit(solution)/shard_map/ppermute | solution.py:31
  40.6 1.7 %fetch.3.refs_7_ = bf16[256,5120]{1,0:T(8,128)(2,1)S(1)} custom-call(bf16[640,5120]{1,0:T(8,128)(2,1)} %w_hbm.5), custom_call_target="tpu_custom_call" | custom-call | bytes 4194304 | tf_op jit(solution)/shard_map/fetch/pallas_call | solution.py:156
  42.4 1.8 %fetch.2.refs_6_ = bf16[256,5120]{1,0:T(8,128)(2,1)S(1)} custom-call(bf16[640,5120]{1,0:T(8,128)(2,1)} %w_hbm.5), custom_call_target="tpu_custom_call" | custom-call | bytes 4194304 | tf_op jit(solution)/shard_map/fetch/pallas_call | solution.py:156
  44.1 0.3 collective-permute-done.12.refs_2_
  44.5 1.1 %project.1 = bf16[8,16,640]{2,1,0:T(8,128)(2,1)S(1)} custom-call(bf16[80,128]{1,0:T(8,128)(2,1)S(1)} %get-tuple-element.21.refs_0_, bf16[80,128]{1,0:T(8,128)(2,1)S(1)} %collective-permute-done.11.refs_1_, bf16[80,128]{1,0:T(8,128)(2,1)S(1)} %collective-permute-done.12.refs_2_, bf16[80,128]{1,0:T(8,128)(2,1)S(1)} %collective-permute-done.13.refs_3_, ...), custom_call_target="tpu_custom_call" | custom-call | tf_op jit(solution)/shard_map/project/pallas_call | solution.py:221
  45.5 12.3 %all_to_all.5 = bf16[8,16,640]{2,1,0:T(8,128)(2,1)S(1)} all-to-all(bf16[8,16,640]{2,1,0:T(8,128)(2,1)S(1)} %project.1), channel_id=1, replica_groups=mesh['seq'=32,'head'=8] {'head'}, dimensions={0} | all-to-all | bytes 327680 | tf_op jit(solution)/shard_map/all_to_all | solution.py:266
  57.8 0.6 %reduce_sum.12 = bf16[16,640]{1,0:T(8,128)(2,1)} reduce(bf16[8,16,640]{2,1,0:T(8,128)(2,1)S(1)} %all_to_all.5, bf16[]{:T(256)} %constant.2.clone.1), dimensions={0}, to_apply=%region_0.0 | reduce | flops 71680 | bytes 184322 | tf_op jit(solution)/shard_map/reduce_sum | solution.py:267
  (17 shorter events, 0.3 us)
Async XLA Ops:
  0.0 21.8 %collective-permute-start.3 = (bf16[2048,128]{1,0:T(8,128)(2,1)}, bf16[2048,128]{1,0:T(8,128)(2,1)S(1)}, u32[]{:S(2)}, u32[]{:S(2)}) collective-permute-start(bf16[2048,128]{1,0:T(8,128)(2,1)} %bitcast.6), channel_id=1, source_target_pairs={{0,8},{8,0},{16,24},{24,16},{32,40},{40,32},{48,56},{56,48},{64,72... | collective-permute-start | bytes 1572872 | tf_op jit(solution)/shard_map/ppermute | solution.py:242
  0.0 2.3 %copy-start = (bf16[16,5,128]{2,0,1:T(8,128)(2,1)S(1)}, bf16[16,5,128]{2,0,1:T(8,128)(2,1)}, u32[]{:S(2)}) copy-start(bf16[16,5,128]{2,0,1:T(8,128)(2,1)} %param.5) | copy-start | bytes 61444
  1.7 20.1 %collective-permute-start.4 = (bf16[128,2048]{1,0:T(8,128)(2,1)S(1)}, bf16[128,2048]{1,0:T(8,128)(2,1)S(1)}, u32[]{:S(2)}, u32[]{:S(2)}) collective-permute-start(bf16[128,2048]{1,0:T(8,128)(2,1)S(1)} %get-tuple-element.18.refs_2_.refs_3_), channel_id=1, source_target_pairs={{0,8},{8,0},{16,24},{24,16},{32,40},{40,32},{48,56},{56,48},{64,72... | collective-permute-start | bytes 1572872 | tf_op jit(solution)/shard_map/ppermute | solution.py:246
  2.3 7.6 %collective-permute-start.2 = (bf16[80,128]{1,0:T(8,128)(2,1)S(1)}, bf16[80,128]{1,0:T(8,128)(2,1)S(1)}, u32[]{:S(2)}, u32[]{:S(2)}) collective-permute-start(bf16[80,128]{1,0:T(8,128)(2,1)S(1)} %bitcast.9), channel_id=1, source_target_pairs={{0,200},{8,192},{16,216},{24,208},{32,232},{40,224},{48,248},{56,2... | collective-permute-start | bytes 61448 | tf_op jit(solution)/shard_map/ppermute | solution.py:31
  7.4 7.1 %collective-permute-start.1 = (bf16[80,128]{1,0:T(8,128)(2,1)S(1)}, bf16[80,128]{1,0:T(8,128)(2,1)S(1)}, u32[]{:S(2)}, u32[]{:S(2)}) collective-permute-start(bf16[80,128]{1,0:T(8,128)(2,1)S(1)} %bitcast.10), channel_id=1, source_target_pairs={{0,136},{8,128},{16,152},{24,144},{32,168},{40,160},{48,184},{56,1... | collective-permute-start | bytes 61448 | tf_op jit(solution)/shard_map/ppermute | solution.py:31
  8.9 5.7 %collective-permute-start = (bf16[80,128]{1,0:T(8,128)(2,1)S(1)}, bf16[80,128]{1,0:T(8,128)(2,1)S(1)}, u32[]{:S(2)}, u32[]{:S(2)}) collective-permute-start(bf16[80,128]{1,0:T(8,128)(2,1)S(1)} %bitcast.11), channel_id=1, source_target_pairs={{0,64},{8,72},{16,80},{24,88},{32,96},{40,104},{48,112},{56,120},{... | collective-permute-start | bytes 61448 | tf_op jit(solution)/shard_map/ppermute | solution.py:31
  14.6 4.2 %collective-permute-start.8 = (bf16[4,80,128]{2,1,0:T(8,128)(2,1)S(1)}, bf16[4,80,128]{2,1,0:T(8,128)(2,1)S(1)}, u32[]{:S(2)}, u32[]{:S(2)}) collective-permute-start(bf16[4,80,128]{2,1,0:T(8,128)(2,1)S(1)} %join.1.refs_0_), channel_id=1, source_target_pairs={{0,24},{8,16},{16,8},{24,0},{32,56},{40,48},{48,40},{56,32},{64,88... | collective-permute-start | bytes 245768 | tf_op jit(solution)/shard_map/ppermute | solution.py:31
  16.2 5.7 %collective-permute-start.7 = (bf16[4,80,128]{2,1,0:T(8,128)(2,1)S(1)}, bf16[4,80,128]{2,1,0:T(8,128)(2,1)S(1)}, u32[]{:S(2)}, u32[]{:S(2)}) collective-permute-start(bf16[4,80,128]{2,1,0:T(8,128)(2,1)S(1)} %join.1.refs_0_), channel_id=1, source_target_pairs={{0,48},{8,56},{16,32},{24,40},{32,16},{40,24},{48,0},{56,8},{64,11... | collective-permute-start | bytes 245768 | tf_op jit(solution)/shard_map/ppermute | solution.py:31
  18.3 8.2 %collective-permute-start.5 = (bf16[4,80,128]{2,1,0:T(8,128)(2,1)S(1)}, bf16[4,80,128]{2,1,0:T(8,128)(2,1)S(1)}, u32[]{:S(2)}, u32[]{:S(2)}) collective-permute-start(bf16[4,80,128]{2,1,0:T(8,128)(2,1)S(1)} %join.1.refs_0_), channel_id=1, source_target_pairs={{0,40},{8,32},{16,56},{24,48},{32,8},{40,0},{48,24},{56,16},{64,10... | collective-permute-start | bytes 245768 | tf_op jit(solution)/shard_map/ppermute | solution.py:31
  24.2 7.7 %collective-permute-start.9 = (bf16[4,80,128]{2,1,0:T(8,128)(2,1)S(1)}, bf16[4,80,128]{2,1,0:T(8,128)(2,1)S(1)}, u32[]{:S(2)}, u32[]{:S(2)}) collective-permute-start(bf16[4,80,128]{2,1,0:T(8,128)(2,1)S(1)} %get-tuple-element.19), channel_id=1, source_target_pairs={{0,48},{8,56},{16,32},{24,40},{32,16},{40,24},{48,0},{56,8},{64,11... | collective-permute-start | bytes 245768 | tf_op jit(solution)/shard_map/ppermute | solution.py:31
  26.4 5.6 %collective-permute-start.10 = (bf16[4,80,128]{2,1,0:T(8,128)(2,1)S(1)}, bf16[4,80,128]{2,1,0:T(8,128)(2,1)S(1)}, u32[]{:S(2)}, u32[]{:S(2)}) collective-permute-start(bf16[4,80,128]{2,1,0:T(8,128)(2,1)S(1)} %get-tuple-element.20), channel_id=1, source_target_pairs={{0,24},{8,16},{16,8},{24,0},{32,56},{40,48},{48,40},{56,32},{64,88... | collective-permute-start | bytes 245768 | tf_op jit(solution)/shard_map/ppermute | solution.py:31
  28.0 6.0 %collective-permute-start.6 = (bf16[4,80,128]{2,1,0:T(8,128)(2,1)S(1)}, bf16[4,80,128]{2,1,0:T(8,128)(2,1)S(1)}, u32[]{:S(2)}, u32[]{:S(2)}) collective-permute-start(bf16[4,80,128]{2,1,0:T(8,128)(2,1)S(1)} %read.4), channel_id=1, source_target_pairs={{0,40},{8,32},{16,56},{24,48},{32,8},{40,0},{48,24},{56,16},{64,10... | collective-permute-start | bytes 245768 | tf_op jit(solution)/shard_map/ppermute | solution.py:31
  34.1 10.0 %collective-permute-start.11 = (bf16[80,128]{1,0:T(8,128)(2,1)S(1)}, bf16[80,128]{1,0:T(8,128)(2,1)S(1)}, u32[]{:S(2)}, u32[]{:S(2)}) collective-permute-start(bf16[80,128]{1,0:T(8,128)(2,1)S(1)} %get-tuple-element.22), channel_id=1, source_target_pairs={{0,136},{8,128},{16,152},{24,144},{32,168},{40,160},{48,184},{56,1... | collective-permute-start | bytes 61448 | tf_op jit(solution)/shard_map/ppermute | solution.py:31
  39.2 5.3 %collective-permute-start.12 = (bf16[80,128]{1,0:T(8,128)(2,1)S(1)}, bf16[80,128]{1,0:T(8,128)(2,1)S(1)}, u32[]{:S(2)}, u32[]{:S(2)}) collective-permute-start(bf16[80,128]{1,0:T(8,128)(2,1)S(1)} %get-tuple-element.23), channel_id=1, source_target_pairs={{0,200},{8,192},{16,216},{24,208},{32,232},{40,224},{48,248},{56,2... | collective-permute-start | bytes 61448 | tf_op jit(solution)/shard_map/ppermute | solution.py:31
  39.2 5.3 %collective-permute-start.13 = (bf16[80,128]{1,0:T(8,128)(2,1)S(1)}, bf16[80,128]{1,0:T(8,128)(2,1)S(1)}, u32[]{:S(2)}, u32[]{:S(2)}) collective-permute-start(bf16[80,128]{1,0:T(8,128)(2,1)S(1)} %get-tuple-element.24), channel_id=1, source_target_pairs={{0,64},{8,72},{16,80},{24,88},{32,96},{40,104},{48,112},{56,120},{... | collective-permute-start | bytes 61448 | tf_op jit(solution)/shard_map/ppermute | solution.py:31

commit v6 on v5

--- a/solution.py
+++ b/solution.py
@@ -13,7 +13,7 @@
 X_CHIPS, Z_BLOCKS, CORES = 4, 4, 2
 ORDER = (2, 3, 1)
 GROUPS = ((0,), (2,), (3, 1))
-Z_FLIPS = (0, 0, 1, 1)
+Z_FLIPS = (0, 0, 1, 0)
 X_FLIPS = (0, 1, 1, 0)
 
 
@@ -226,6 +226,21 @@
         compiler_params=params(24),
         name="project",
     )(*parts, gain, *weights)
+
+
+def sum_kernel(p_ref, o_ref):
+    o_ref[...] = jnp.sum(p_ref[...].astype(jnp.float32), axis=0).astype(o_ref.dtype)
+
+
+def sum_pieces(pieces):
+    return pl.pallas_call(
+        sum_kernel,
+        out_shape=jax.ShapeDtypeStruct(pieces.shape[1:], pieces.dtype),
+        in_specs=[VMEM],
+        out_specs=VMEM,
+        compiler_params=params(2),
+        name="sum_pieces",
+    )(pieces)
 
 
 def layer(queries, document_key_rows, document_value_rows, out_gain, out_weight):
@@ -264,7 +279,7 @@
         parts.append(exchange(slots[steps], steps, 0, Z_FLIPS[steps]))
     projected = project(parts, gain, weights, head_groups)
     pieces = lax.all_to_all(projected, "head", 0, 0, tiled=True)
-    return jnp.sum(pieces.astype(jnp.float32), axis=0).astype(jnp.bfloat16)
+    return sum_pieces(pieces)
 
 
 def solution(mesh):

time: 59.2 us -> 60.6 us (1.024)
  the two profiles are of different devices: /device:TPU:32 before, /device:TPU:2 now
where the time goes in v6:
time: 60.6 us; the launch traced here: 60.4 us
  starting transfers between devices  26.6 us (44%)
  Pallas kernels  12.5 us (21%)
  blocking collectives  11.6 us (19%)
  waiting for transfers between devices  9.6 us (16%)
    ppermute x12, starting transfers between devices, exchange(): return lax.ppermute(rows, 'seq', pairs)  26 us
    all_to_all x1, blocking collectives, layer(): pieces = lax.all_to_all(projected, 'head', 0, 0, tiled=True)  11.6 us
    ppermute x12, waiting for transfers between devices, exchange(): return lax.ppermute(rows, 'seq', pairs)  9.59 us
    pallas_call x3, Pallas kernels, read(): pl.pallas_call(functools.partial(read_kernel, len(chunks)), out_shape=(ou...  5.55 us
    pallas_call x2, Pallas kernels, fetch(): pl.pallas_call(functools.partial(fetch_kernel, first_row), out_shape=jax....  3.5 us
    pallas_call x1, Pallas kernels, stage(): pl.pallas_call(stage_kernel, out_shape=(like(rows), like(keys), like(valu...  1.72 us
  transfers between devices with their start and end apart: 14, of which 4 were waited for; matrix products, arithmetic and copies ran while one was open for 0% of the time, Pallas kernels for 18%

profile of v6, /device:TPU:2, one launch (start us, length us, event | category | flops | bytes accessed | tf_op | source)
XLA Modules:
  0.0 60.4 jit_solution(3444011881957630028)
XLA Ops:
  0.0 1.7 %stage.1 = (bf16[80,128]{1,0:T(8,128)(2,1)S(1)}, bf16[2048,128]{1,0:T(8,128)(2,1)S(1)}, bf16[128,2048]{1,0:T(8,128)(2,1)S(1)}, f32[5,128]{1,0:T(8,128)S(1)}, bf16[128,5120]{1,0:T(8,128)(2,1)S(1)}) custom-call(bf16[80,128]{1,0:T(8,128)(2,1)} %bitcast.8, bf16[2048,128]{1,0:T(8,128)(2,1)} %bitcast.7, bf16[2048,128]{1,0:T(8,128)(2,1)} %bitcast.5, ...), custom_call_target="tpu_custom_call" | custom-call | bytes 4194304 | tf_op jit(solution)/shard_map/stage/pallas_call | solution.py:70
  1.7 0.6 collective-permute-start.4
  2.3 6.3 %collective-permute-start.2 = (bf16[80,128]{1,0:T(8,128)(2,1)S(1)}, bf16[80,128]{1,0:T(8,128)(2,1)S(1)}, u32[]{:S(2)}, u32[]{:S(2)}) collective-permute-start(bf16[80,128]{1,0:T(8,128)(2,1)S(1)} %bitcast.9), channel_id=1, source_target_pairs={{0,192},{8,200},{16,208},{24,216},{32,224},{40,232},{48,240},{56,2... | collective-permute-start | bytes 61448 | tf_op jit(solution)/shard_map/ppermute | solution.py:31
  8.6 0.7 %collective-permute-start.1 = (bf16[80,128]{1,0:T(8,128)(2,1)S(1)}, bf16[80,128]{1,0:T(8,128)(2,1)S(1)}, u32[]{:S(2)}, u32[]{:S(2)}) collective-permute-start(bf16[80,128]{1,0:T(8,128)(2,1)S(1)} %bitcast.10), channel_id=1, source_target_pairs={{0,136},{8,128},{16,152},{24,144},{32,168},{40,160},{48,184},{56,1... | collective-permute-start | bytes 61448 | tf_op jit(solution)/shard_map/ppermute | solution.py:31
  9.3 1.5 %collective-permute-start = (bf16[80,128]{1,0:T(8,128)(2,1)S(1)}, bf16[80,128]{1,0:T(8,128)(2,1)S(1)}, u32[]{:S(2)}, u32[]{:S(2)}) collective-permute-start(bf16[80,128]{1,0:T(8,128)(2,1)S(1)} %bitcast.11), channel_id=1, source_target_pairs={{0,64},{8,72},{16,80},{24,88},{32,96},{40,104},{48,112},{56,120},{... | collective-permute-start | bytes 61448 | tf_op jit(solution)/shard_map/ppermute | solution.py:31
  10.8 5.2 %collective-permute-done.1.refs_2_ = bf16[80,128]{1,0:T(8,128)(2,1)S(1)} collective-permute-done((bf16[80,128]{1,0:T(8,128)(2,1)S(1)}, bf16[80,128]{1,0:T(8,128)(2,1)S(1)}, u32[]{:S(2)}, u32[]{:S(2)}) %collective-permute-start.1) | collective-permute-done | bytes 20512 | tf_op jit(solution)/shard_map/ppermute | solution.py:31
  16.4 2.2 %collective-permute-start.7 = (bf16[4,80,128]{2,1,0:T(8,128)(2,1)S(1)}, bf16[4,80,128]{2,1,0:T(8,128)(2,1)S(1)}, u32[]{:S(2)}, u32[]{:S(2)}) collective-permute-start(bf16[4,80,128]{2,1,0:T(8,128)(2,1)S(1)} %join.1.refs_0_), channel_id=1, source_target_pairs={{0,48},{8,56},{16,32},{24,40},{32,16},{40,24},{48,0},{56,8},{64,11... | collective-permute-start | bytes 245768 | tf_op jit(solution)/shard_map/ppermute | solution.py:31
  18.5 1.1 %collective-permute-start.5 = (bf16[4,80,128]{2,1,0:T(8,128)(2,1)S(1)}, bf16[4,80,128]{2,1,0:T(8,128)(2,1)S(1)}, u32[]{:S(2)}, u32[]{:S(2)}) collective-permute-start(bf16[4,80,128]{2,1,0:T(8,128)(2,1)S(1)} %join.1.refs_0_), channel_id=1, source_target_pairs={{0,40},{8,32},{16,56},{24,48},{32,8},{40,0},{48,24},{56,16},{64,10... | collective-permute-start | bytes 245768 | tf_op jit(solution)/shard_map/ppermute | solution.py:31
  19.6 0.9 %collective-permute-done.8.refs_1_ = bf16[4,80,128]{2,1,0:T(8,128)(2,1)S(1)} collective-permute-done((bf16[4,80,128]{2,1,0:T(8,128)(2,1)S(1)}, bf16[4,80,128]{2,1,0:T(8,128)(2,1)S(1)}, u32[]{:S(2)}, u32[]{:S(2)}) %collective-permute-start.8) | collective-permute-done | bytes 81952 | tf_op jit(solution)/shard_map/ppermute | solution.py:31
  20.6 1.0 %collective-permute-done.7.refs_0_ = bf16[4,80,128]{2,1,0:T(8,128)(2,1)S(1)} collective-permute-done((bf16[4,80,128]{2,1,0:T(8,128)(2,1)S(1)}, bf16[4,80,128]{2,1,0:T(8,128)(2,1)S(1)}, u32[]{:S(2)}, u32[]{:S(2)}) %collective-permute-start.7) | collective-permute-done | bytes 81952 | tf_op jit(solution)/shard_map/ppermute | solution.py:31
  21.5 2.4 %read.5 = (bf16[4,80,128]{2,1,0:T(8,128)(2,1)S(1)}, bf16[4,80,128]{2,1,0:T(8,128)(2,1)S(1)}) custom-call(bf16[4,80,128]{2,1,0:T(8,128)(2,1)S(1)} %collective-permute-done.7.refs_0_, bf16[4,80,128]{2,1,0:T(8,128)(2,1)S(1)} %collective-permute-done.8.refs_1_, bf16[2048,128]{1,0:T(8,128)(2,1)S(1)} %get-tuple-element.17.refs_1_.refs_2_, ...), custom_call_target="tpu_custom_call" | custom-call | flops 1342177280 | bytes 4194304 | tf_op jit(solution)/shard_map/read/pallas_call | solution.py:136
  23.9 3.6 %collective-permute-start.9 = (bf16[4,80,128]{2,1,0:T(8,128)(2,1)S(1)}, bf16[4,80,128]{2,1,0:T(8,128)(2,1)S(1)}, u32[]{:S(2)}, u32[]{:S(2)}) collective-permute-start(bf16[4,80,128]{2,1,0:T(8,128)(2,1)S(1)} %get-tuple-element.19), channel_id=1, source_target_pairs={{0,48},{8,56},{16,32},{24,40},{32,16},{40,24},{48,0},{56,8},{64,11... | collective-permute-start | bytes 245768 | tf_op jit(solution)/shard_map/ppermute | solution.py:31
  27.5 1.6 %read.4 = bf16[4,80,128]{2,1,0:T(8,128)(2,1)S(1)} custom-call(bf16[4,80,128]{2,1,0:T(8,128)(2,1)S(1)} %collective-permute-done.5.refs_0_, bf16[2048,128]{1,0:T(8,128)(2,1)S(1)} %get-tuple-element.17.refs_1_.refs_2_, bf16[128,2048]{1,0:T(8,128)(2,1)S(1)} %get-tuple-element.18.refs_2_.refs_3_, bf16[2048,128]{1,0:T(8,128)(2,1)S(1)} %collective-permute-done.3.refs_3_.refs_4_, ...), custom_call_target="tpu_custom_call" | custom-call | flops 671088640 | bytes 4194304 | tf_op jit(solution)/shard_map/read/pallas_call | solution.py:136
  29.1 1.4 %collective-permute-start.6 = (bf16[4,80,128]{2,1,0:T(8,128)(2,1)S(1)}, bf16[4,80,128]{2,1,0:T(8,128)(2,1)S(1)}, u32[]{:S(2)}, u32[]{:S(2)}) collective-permute-start(bf16[4,80,128]{2,1,0:T(8,128)(2,1)S(1)} %read.4), channel_id=1, source_target_pairs={{0,40},{8,32},{16,56},{24,48},{32,8},{40,0},{48,24},{56,16},{64,10... | collective-permute-start | bytes 245768 | tf_op jit(solution)/shard_map/ppermute | solution.py:31
  30.5 1.6 %read.3.refs_0_ = bf16[4,80,128]{2,1,0:T(8,128)(2,1)S(1)} custom-call(bf16[4,80,128]{2,1,0:T(8,128)(2,1)S(1)} %join.1.refs_0_, bf16[2048,128]{1,0:T(8,128)(2,1)S(1)} %get-tuple-element.17.refs_1_.refs_2_, bf16[128,2048]{1,0:T(8,128)(2,1)S(1)} %get-tuple-element.18.refs_2_.refs_3_, bf16[2048,128]{1,0:T(8,128)(2,1)S(1)} %collective-permute-done.3.refs_3_.refs_4_, ...), custom_call_target="tpu_custom_call" | custom-call | flops 671088640 | bytes 4194304 | tf_op jit(solution)/shard_map/read/pallas_call | solution.py:136
  32.1 2.5 %collective-permute-done.6.refs_1_ = bf16[4,80,128]{2,1,0:T(8,128)(2,1)S(1)} collective-permute-done((bf16[4,80,128]{2,1,0:T(8,128)(2,1)S(1)}, bf16[4,80,128]{2,1,0:T(8,128)(2,1)S(1)}, u32[]{:S(2)}, u32[]{:S(2)}) %collective-permute-start.6) | collective-permute-done | bytes 81952 | tf_op jit(solution)/shard_map/ppermute | solution.py:31
  34.6 5.5 %collective-permute-start.11 = (bf16[80,128]{1,0:T(8,128)(2,1)S(1)}, bf16[80,128]{1,0:T(8,128)(2,1)S(1)}, u32[]{:S(2)}, u32[]{:S(2)}) collective-permute-start(bf16[80,128]{1,0:T(8,128)(2,1)S(1)} %get-tuple-element.22), channel_id=1, source_target_pairs={{0,136},{8,128},{16,152},{24,144},{32,168},{40,160},{48,184},{56,1... | collective-permute-start | bytes 61448 | tf_op jit(solution)/shard_map/ppermute | solution.py:31
  40.1 1.9 %collective-permute-start.12 = (bf16[80,128]{1,0:T(8,128)(2,1)S(1)}, bf16[80,128]{1,0:T(8,128)(2,1)S(1)}, u32[]{:S(2)}, u32[]{:S(2)}) collective-permute-start(bf16[80,128]{1,0:T(8,128)(2,1)S(1)} %get-tuple-element.23), channel_id=1, source_target_pairs={{0,192},{8,200},{16,208},{24,216},{32,224},{40,232},{48,240},{56,2... | collective-permute-start | bytes 61448 | tf_op jit(solution)/shard_map/ppermute | solution.py:31
  42.0 1.5 %collective-permute-start.13 = (bf16[80,128]{1,0:T(8,128)(2,1)S(1)}, bf16[80,128]{1,0:T(8,128)(2,1)S(1)}, u32[]{:S(2)}, u32[]{:S(2)}) collective-permute-start(bf16[80,128]{1,0:T(8,128)(2,1)S(1)} %get-tuple-element.24), channel_id=1, source_target_pairs={{0,64},{8,72},{16,80},{24,88},{32,96},{40,104},{48,112},{56,120},{... | collective-permute-start | bytes 61448 | tf_op jit(solution)/shard_map/ppermute | solution.py:31
  43.6 1.7 %fetch.3.refs_7_ = bf16[256,5120]{1,0:T(8,128)(2,1)S(1)} custom-call(bf16[640,5120]{1,0:T(8,128)(2,1)} %w_hbm.5), custom_call_target="tpu_custom_call" | custom-call | bytes 4194304 | tf_op jit(solution)/shard_map/fetch/pallas_call | solution.py:156
  45.3 1.8 %fetch.2.refs_6_ = bf16[256,5120]{1,0:T(8,128)(2,1)S(1)} custom-call(bf16[640,5120]{1,0:T(8,128)(2,1)} %w_hbm.5), custom_call_target="tpu_custom_call" | custom-call | bytes 4194304 | tf_op jit(solution)/shard_map/fetch/pallas_call | solution.py:156
  47.1 1.1 %project.1 = bf16[8,16,640]{2,1,0:T(8,128)(2,1)S(1)} custom-call(bf16[80,128]{1,0:T(8,128)(2,1)S(1)} %get-tuple-element.21.refs_0_, bf16[80,128]{1,0:T(8,128)(2,1)S(1)} %collective-permute-done.11.refs_1_, bf16[80,128]{1,0:T(8,128)(2,1)S(1)} %collective-permute-done.12.refs_2_, bf16[80,128]{1,0:T(8,128)(2,1)S(1)} %collective-permute-done.13.refs_3_, ...), custom_call_target="tpu_custom_call" | custom-call | tf_op jit(solution)/shard_map/project/pallas_call | solution.py:221
  48.2 11.6 %all_to_all.5.p_ref = bf16[8,16,640]{2,1,0:T(8,128)(2,1)S(1)} all-to-all(bf16[8,16,640]{2,1,0:T(8,128)(2,1)S(1)} %project.1), channel_id=1, replica_groups=mesh['seq'=32,'head'=8] {'head'}, dimensions={0} | all-to-all | bytes 327680 | tf_op jit(solution)/shard_map/all_to_all | solution.py:281
  59.8 0.6 %sum_pieces.1 = bf16[16,640]{1,0:T(8,128)(2,1)} custom-call(bf16[8,16,640]{2,1,0:T(8,128)(2,1)S(1)} %all_to_all.5.p_ref), custom_call_target="tpu_custom_call" | custom-call | tf_op jit(solution)/shard_map/sum_pieces/pallas_call | solution.py:236
  (17 shorter events, 0.4 us)
Async XLA Ops:
  0.0 21.5 %collective-permute-start.3 = (bf16[2048,128]{1,0:T(8,128)(2,1)}, bf16[2048,128]{1,0:T(8,128)(2,1)S(1)}, u32[]{:S(2)}, u32[]{:S(2)}) collective-permute-start(bf16[2048,128]{1,0:T(8,128)(2,1)} %bitcast.6), channel_id=1, source_target_pairs={{0,8},{8,0},{16,24},{24,16},{32,40},{40,32},{48,56},{56,48},{64,72... | collective-permute-start | bytes 1572872 | tf_op jit(solution)/shard_map/ppermute | solution.py:257
  0.0 2.3 %copy-start = (bf16[16,5,128]{2,0,1:T(8,128)(2,1)S(1)}, bf16[16,5,128]{2,0,1:T(8,128)(2,1)}, u32[]{:S(2)}) copy-start(bf16[16,5,128]{2,0,1:T(8,128)(2,1)} %param.5) | copy-start | bytes 61444
  1.7 19.8 %collective-permute-start.4 = (bf16[128,2048]{1,0:T(8,128)(2,1)S(1)}, bf16[128,2048]{1,0:T(8,128)(2,1)S(1)}, u32[]{:S(2)}, u32[]{:S(2)}) collective-permute-start(bf16[128,2048]{1,0:T(8,128)(2,1)S(1)} %get-tuple-element.18.refs_2_.refs_3_), channel_id=1, source_target_pairs={{0,8},{8,0},{16,24},{24,16},{32,40},{40,32},{48,56},{56,48},{64,72... | collective-permute-start | bytes 1572872 | tf_op jit(solution)/shard_map/ppermute | solution.py:261
  2.3 8.5 %collective-permute-start.2 = (bf16[80,128]{1,0:T(8,128)(2,1)S(1)}, bf16[80,128]{1,0:T(8,128)(2,1)S(1)}, u32[]{:S(2)}, u32[]{:S(2)}) collective-permute-start(bf16[80,128]{1,0:T(8,128)(2,1)S(1)} %bitcast.9), channel_id=1, source_target_pairs={{0,192},{8,200},{16,208},{24,216},{32,224},{40,232},{48,240},{56,2... | collective-permute-start | bytes 61448 | tf_op jit(solution)/shard_map/ppermute | solution.py:31
  8.6 7.4 %collective-permute-start.1 = (bf16[80,128]{1,0:T(8,128)(2,1)S(1)}, bf16[80,128]{1,0:T(8,128)(2,1)S(1)}, u32[]{:S(2)}, u32[]{:S(2)}) collective-permute-start(bf16[80,128]{1,0:T(8,128)(2,1)S(1)} %bitcast.10), channel_id=1, source_target_pairs={{0,136},{8,128},{16,152},{24,144},{32,168},{40,160},{48,184},{56,1... | collective-permute-start | bytes 61448 | tf_op jit(solution)/shard_map/ppermute | solution.py:31
  9.3 6.7 %collective-permute-start = (bf16[80,128]{1,0:T(8,128)(2,1)S(1)}, bf16[80,128]{1,0:T(8,128)(2,1)S(1)}, u32[]{:S(2)}, u32[]{:S(2)}) collective-permute-start(bf16[80,128]{1,0:T(8,128)(2,1)S(1)} %bitcast.11), channel_id=1, source_target_pairs={{0,64},{8,72},{16,80},{24,88},{32,96},{40,104},{48,112},{56,120},{... | collective-permute-start | bytes 61448 | tf_op jit(solution)/shard_map/ppermute | solution.py:31
  16.0 4.5 %collective-permute-start.8 = (bf16[4,80,128]{2,1,0:T(8,128)(2,1)S(1)}, bf16[4,80,128]{2,1,0:T(8,128)(2,1)S(1)}, u32[]{:S(2)}, u32[]{:S(2)}) collective-permute-start(bf16[4,80,128]{2,1,0:T(8,128)(2,1)S(1)} %join.1.refs_0_), channel_id=1, source_target_pairs={{0,24},{8,16},{16,8},{24,0},{32,56},{40,48},{48,40},{56,32},{64,88... | collective-permute-start | bytes 245768 | tf_op jit(solution)/shard_map/ppermute | solution.py:31
  16.4 5.2 %collective-permute-start.7 = (bf16[4,80,128]{2,1,0:T(8,128)(2,1)S(1)}, bf16[4,80,128]{2,1,0:T(8,128)(2,1)S(1)}, u32[]{:S(2)}, u32[]{:S(2)}) collective-permute-start(bf16[4,80,128]{2,1,0:T(8,128)(2,1)S(1)} %join.1.refs_0_), channel_id=1, source_target_pairs={{0,48},{8,56},{16,32},{24,40},{32,16},{40,24},{48,0},{56,8},{64,11... | collective-permute-start | bytes 245768 | tf_op jit(solution)/shard_map/ppermute | solution.py:31
  18.5 9.0 %collective-permute-start.5 = (bf16[4,80,128]{2,1,0:T(8,128)(2,1)S(1)}, bf16[4,80,128]{2,1,0:T(8,128)(2,1)S(1)}, u32[]{:S(2)}, u32[]{:S(2)}) collective-permute-start(bf16[4,80,128]{2,1,0:T(8,128)(2,1)S(1)} %join.1.refs_0_), channel_id=1, source_target_pairs={{0,40},{8,32},{16,56},{24,48},{32,8},{40,0},{48,24},{56,16},{64,10... | collective-permute-start | bytes 245768 | tf_op jit(solution)/shard_map/ppermute | solution.py:31
  23.9 8.1 %collective-permute-start.9 = (bf16[4,80,128]{2,1,0:T(8,128)(2,1)S(1)}, bf16[4,80,128]{2,1,0:T(8,128)(2,1)S(1)}, u32[]{:S(2)}, u32[]{:S(2)}) collective-permute-start(bf16[4,80,128]{2,1,0:T(8,128)(2,1)S(1)} %get-tuple-element.19), channel_id=1, source_target_pairs={{0,48},{8,56},{16,32},{24,40},{32,16},{40,24},{48,0},{56,8},{64,11... | collective-permute-start | bytes 245768 | tf_op jit(solution)/shard_map/ppermute | solution.py:31
  27.5 4.5 %collective-permute-start.10 = (bf16[4,80,128]{2,1,0:T(8,128)(2,1)S(1)}, bf16[4,80,128]{2,1,0:T(8,128)(2,1)S(1)}, u32[]{:S(2)}, u32[]{:S(2)}) collective-permute-start(bf16[4,80,128]{2,1,0:T(8,128)(2,1)S(1)} %get-tuple-element.20), channel_id=1, source_target_pairs={{0,24},{8,16},{16,8},{24,0},{32,56},{40,48},{48,40},{56,32},{64,88... | collective-permute-start | bytes 245768 | tf_op jit(solution)/shard_map/ppermute | solution.py:31
  29.1 5.5 %collective-permute-start.6 = (bf16[4,80,128]{2,1,0:T(8,128)(2,1)S(1)}, bf16[4,80,128]{2,1,0:T(8,128)(2,1)S(1)}, u32[]{:S(2)}, u32[]{:S(2)}) collective-permute-start(bf16[4,80,128]{2,1,0:T(8,128)(2,1)S(1)} %read.4), channel_id=1, source_target_pairs={{0,40},{8,32},{16,56},{24,48},{32,8},{40,0},{48,24},{56,16},{64,10... | collective-permute-start | bytes 245768 | tf_op jit(solution)/shard_map/ppermute | solution.py:31
  34.6 12.5 %collective-permute-start.11 = (bf16[80,128]{1,0:T(8,128)(2,1)S(1)}, bf16[80,128]{1,0:T(8,128)(2,1)S(1)}, u32[]{:S(2)}, u32[]{:S(2)}) collective-permute-start(bf16[80,128]{1,0:T(8,128)(2,1)S(1)} %get-tuple-element.22), channel_id=1, source_target_pairs={{0,136},{8,128},{16,152},{24,144},{32,168},{40,160},{48,184},{56,1... | collective-permute-start | bytes 61448 | tf_op jit(solution)/shard_map/ppermute | solution.py:31
  40.1 6.9 %collective-permute-start.12 = (bf16[80,128]{1,0:T(8,128)(2,1)S(1)}, bf16[80,128]{1,0:T(8,128)(2,1)S(1)}, u32[]{:S(2)}, u32[]{:S(2)}) collective-permute-start(bf16[80,128]{1,0:T(8,128)(2,1)S(1)} %get-tuple-element.23), channel_id=1, source_target_pairs={{0,192},{8,200},{16,208},{24,216},{32,224},{40,232},{48,240},{56,2... | collective-permute-start | bytes 61448 | tf_op jit(solution)/shard_map/ppermute | solution.py:31
  42.0 5.1 %collective-permute-start.13 = (bf16[80,128]{1,0:T(8,128)(2,1)S(1)}, bf16[80,128]{1,0:T(8,128)(2,1)S(1)}, u32[]{:S(2)}, u32[]{:S(2)}) collective-permute-start(bf16[80,128]{1,0:T(8,128)(2,1)S(1)} %get-tuple-element.24), channel_id=1, source_target_pairs={{0,64},{8,72},{16,80},{24,88},{32,96},{40,104},{48,112},{56,120},{... | collective-permute-start | bytes 61448 | tf_op jit(solution)/shard_map/ppermute | solution.py:31

commit v7 on v5

--- a/solution.py
+++ b/solution.py
@@ -44,14 +44,13 @@
 
 
 def stage_kernel(
-    q_hbm, k_hbm, v_hbm, g_hbm, w_hbm, q_ref, k_ref, vt_ref, g_ref, w_ref, v_ref, sems
+    q_hbm, k_hbm, v_hbm, g_hbm, q_ref, k_ref, vt_ref, g_ref, v_ref, sems
 ):
     routes = (
         (v_hbm, v_ref),
         (k_hbm, k_ref),
         (q_hbm, q_ref),
         (g_hbm, g_ref),
-        (w_hbm.at[pl.ds(0, w_ref.shape[0]), :], w_ref),
     )
     copies = [pltpu.make_async_copy(a, b, sems.at[i]) for i, (a, b) in enumerate(routes)]
     for copy in copies:
@@ -63,7 +62,7 @@
         copy.wait()
 
 
-def stage(rows, keys, values, gain, weight, weight_rows):
+def stage(rows, keys, values, gain):
     def like(array, *shape):
         return jax.ShapeDtypeStruct(shape or array.shape, array.dtype)
 
@@ -74,18 +73,17 @@
             like(keys),
             like(values, *values.shape[::-1]),
             like(gain),
-            like(weight, weight_rows, weight.shape[1]),
         ),
-        in_specs=[HBM] * 5,
-        out_specs=(VMEM,) * 5,
+        in_specs=[HBM] * 4,
+        out_specs=(VMEM,) * 4,
         scratch_shapes=[
             pltpu.VMEM(values.shape, values.dtype),
-            pltpu.SemaphoreType.DMA((5,)),
+            pltpu.SemaphoreType.DMA((4,)),
         ],
         compiler_params=params(6),
         cost_estimate=pl.CostEstimate(flops=0, bytes_accessed=4 << 20, transcendentals=0),
         name="stage",
-    )(*(in_hbm(a) for a in (rows, keys, values, gain, weight)))
+    )(*(in_hbm(a) for a in (rows, keys, values, gain)))
 
 
 def join_kernel(*refs):
@@ -240,9 +238,7 @@
         from_z[steps] = exchange(own, steps, 0, Z_FLIPS[steps])
     other_core = [(i, i ^ 1) for i in range(lax.axis_size("seq"))]
     near_keys = lax.ppermute(keys, "seq", other_core)
-    staged_own, staged_keys, staged_turned, gain, weight = stage(
-        own, keys, values, out_gain, out_weight, width
-    )
+    staged_own, staged_keys, staged_turned, gain = stage(own, keys, values, out_gain)
     near_turned = lax.ppermute(staged_turned, "seq", other_core)
     column = join([staged_own, *(from_z[steps] for steps in range(1, Z_BLOCKS))])
     document = (staged_keys, staged_turned, near_keys, near_turned)
@@ -254,10 +250,10 @@
         results = read(tuple(from_x[steps] if steps else column for steps in group), document)
         for steps, result in zip(group, results):
             parts.append(exchange(result, 0, steps, X_FLIPS[steps]) if steps else result)
-    middle = width * (1 + (heads - 1) // 2)
-    middle_weight = fetch(out_weight, width, middle - width)
+    middle = width * (heads // 2)
+    middle_weight = fetch(out_weight, 0, middle)
     last_weight = fetch(out_weight, middle, heads * width - middle)
-    weights = [weight, middle_weight, last_weight]
+    weights = [middle_weight, last_weight]
     slots = add(parts)
     parts = [slots[0]]
     for steps in ORDER:

time: 59.2 us -> 59.4 us (level)
  transfers between devices with their start and end apart: 14 -> 14, of which waited for: 5 -> 4; matrix products, arithmetic and copies ran while one was open for 0% -> 0% of each run, Pallas kernels for 18% -> 18%
where the time goes in v7:
time: 59.4 us; the launch traced here: 58.6 us
  starting transfers between devices  23.3 us (39%)
  blocking collectives  12.6 us (21%)
  Pallas kernels  11.8 us (20%)
  waiting for transfers between devices  10.1 us (17%)
  other arithmetic  0.63 us (1%)
    ppermute x12, starting transfers between devices, exchange(): return lax.ppermute(rows, 'seq', pairs)  22.7 us
    all_to_all x1, blocking collectives, layer(): pieces = lax.all_to_all(projected, 'head', 0, 0, tiled=True)  12.6 us
    ppermute x12, waiting for transfers between devices, exchange(): return lax.ppermute(rows, 'seq', pairs)  10.1 us
    pallas_call x3, Pallas kernels, read(): pl.pallas_call(functools.partial(read_kernel, len(chunks)), out_shape=(ou...  5.55 us
    pallas_call x2, Pallas kernels, fetch(): pl.pallas_call(functools.partial(fetch_kernel, first_row), out_shape=jax....  3.87 us
    pallas_call x1, Pallas kernels, stage(): pl.pallas_call(stage_kernel, out_shape=(like(rows), like(keys), like(valu...  1.27 us
  transfers between devices with their start and end apart: 14, of which 4 were waited for; matrix products, arithmetic and copies ran while one was open for 0% of the time, Pallas kernels for 18%

profile of v7, /device:TPU:32, one launch (start us, length us, event | category | flops | bytes accessed | tf_op | source)
XLA Modules:
  0.0 58.6 jit_solution(4452640028657292242)
XLA Ops:
  0.0 1.3 %stage.1 = (bf16[80,128]{1,0:T(8,128)(2,1)S(1)}, bf16[2048,128]{1,0:T(8,128)(2,1)S(1)}, bf16[128,2048]{1,0:T(8,128)(2,1)S(1)}, f32[5,128]{1,0:T(8,128)S(1)}) custom-call(bf16[80,128]{1,0:T(8,128)(2,1)} %bitcast.8, bf16[2048,128]{1,0:T(8,128)(2,1)} %bitcast.7, bf16[2048,128]{1,0:T(8,128)(2,1)} %bitcast.5, f32[5,128]{1,0:T(8,128)} %g_hbm.1), custom_call_target="tpu_custom_call" | custom-call | bytes 4194304 | tf_op jit(solution)/shard_map/stage/pallas_call | solution.py:69
  1.3 0.6 %collective-permute-start.4 = (bf16[128,2048]{1,0:T(8,128)(2,1)S(1)}, bf16[128,2048]{1,0:T(8,128)(2,1)S(1)}, u32[]{:S(2)}, u32[]{:S(2)}) collective-permute-start(bf16[128,2048]{1,0:T(8,128)(2,1)S(1)} %get-tuple-element.17.refs_2_.refs_3_), channel_id=1, source_target_pairs={{0,8},{8,0},{16,24},{24,16},{32,40},{40,32},{48,56},{56,48},{64,72... | collective-permute-start | bytes 1572872 | tf_op jit(solution)/shard_map/ppermute | solution.py:242
  1.9 5.1 %collective-permute-start.2 = (bf16[80,128]{1,0:T(8,128)(2,1)}, bf16[80,128]{1,0:T(8,128)(2,1)S(1)}, u32[]{:S(2)}, u32[]{:S(2)}) collective-permute-start(bf16[80,128]{1,0:T(8,128)(2,1)} %bitcast.9), channel_id=1, source_target_pairs={{0,200},{8,192},{16,216},{24,208},{32,232},{40,224},{48,248},{56,2... | collective-permute-start | bytes 61448 | tf_op jit(solution)/shard_map/ppermute | solution.py:31
  7.0 1.5 %collective-permute-start.1 = (bf16[80,128]{1,0:T(8,128)(2,1)}, bf16[80,128]{1,0:T(8,128)(2,1)S(1)}, u32[]{:S(2)}, u32[]{:S(2)}) collective-permute-start(bf16[80,128]{1,0:T(8,128)(2,1)} %bitcast.10), channel_id=1, source_target_pairs={{0,136},{8,128},{16,152},{24,144},{32,168},{40,160},{48,184},{56,1... | collective-permute-start | bytes 61448 | tf_op jit(solution)/shard_map/ppermute | solution.py:31
  8.4 1.0 %collective-permute-start = (bf16[80,128]{1,0:T(8,128)(2,1)}, bf16[80,128]{1,0:T(8,128)(2,1)S(1)}, u32[]{:S(2)}, u32[]{:S(2)}) collective-permute-start(bf16[80,128]{1,0:T(8,128)(2,1)} %bitcast.11), channel_id=1, source_target_pairs={{0,64},{8,72},{16,80},{24,88},{32,96},{40,104},{48,112},{56,120},{... | collective-permute-start | bytes 61448 | tf_op jit(solution)/shard_map/ppermute | solution.py:31
  9.4 4.9 %collective-permute-done.1.refs_2_ = bf16[80,128]{1,0:T(8,128)(2,1)S(1)} collective-permute-done((bf16[80,128]{1,0:T(8,128)(2,1)}, bf16[80,128]{1,0:T(8,128)(2,1)S(1)}, u32[]{:S(2)}, u32[]{:S(2)}) %collective-permute-start.1) | collective-permute-done | bytes 20512 | tf_op jit(solution)/shard_map/ppermute | solution.py:31
  14.3 1.6 %collective-permute-start.8 = (bf16[4,80,128]{2,1,0:T(8,128)(2,1)S(1)}, bf16[4,80,128]{2,1,0:T(8,128)(2,1)S(1)}, u32[]{:S(2)}, u32[]{:S(2)}) collective-permute-start(bf16[4,80,128]{2,1,0:T(8,128)(2,1)S(1)} %join.1.refs_0_), channel_id=1, source_target_pairs={{0,24},{8,16},{16,8},{24,0},{32,56},{40,48},{48,40},{56,32},{64,88... | collective-permute-start | bytes 245768 | tf_op jit(solution)/shard_map/ppermute | solution.py:31
  15.9 2.1 %collective-permute-start.7 = (bf16[4,80,128]{2,1,0:T(8,128)(2,1)S(1)}, bf16[4,80,128]{2,1,0:T(8,128)(2,1)S(1)}, u32[]{:S(2)}, u32[]{:S(2)}) collective-permute-start(bf16[4,80,128]{2,1,0:T(8,128)(2,1)S(1)} %join.1.refs_0_), channel_id=1, source_target_pairs={{0,48},{8,56},{16,32},{24,40},{32,16},{40,24},{48,0},{56,8},{64,11... | collective-permute-start | bytes 245768 | tf_op jit(solution)/shard_map/ppermute | solution.py:31
  18.0 0.3 collective-permute-start.5
  18.4 0.2 collective-permute-done.8.refs_1_
  18.6 3.0 %collective-permute-done.7.refs_0_ = bf16[4,80,128]{2,1,0:T(8,128)(2,1)S(1)} collective-permute-done((bf16[4,80,128]{2,1,0:T(8,128)(2,1)S(1)}, bf16[4,80,128]{2,1,0:T(8,128)(2,1)S(1)}, u32[]{:S(2)}, u32[]{:S(2)}) %collective-permute-start.7) | collective-permute-done | bytes 81952 | tf_op jit(solution)/shard_map/ppermute | solution.py:31
  21.6 2.4 %read.5 = (bf16[4,80,128]{2,1,0:T(8,128)(2,1)S(1)}, bf16[4,80,128]{2,1,0:T(8,128)(2,1)S(1)}) custom-call(bf16[4,80,128]{2,1,0:T(8,128)(2,1)S(1)} %collective-permute-done.7.refs_0_, bf16[4,80,128]{2,1,0:T(8,128)(2,1)S(1)} %collective-permute-done.8.refs_1_, bf16[2048,128]{1,0:T(8,128)(2,1)S(1)} %get-tuple-element.16.refs_1_.refs_2_, ...), custom_call_target="tpu_custom_call" | custom-call | flops 1342177280 | bytes 4194304 | tf_op jit(solution)/shard_map/read/pallas_call | solution.py:134
  24.0 2.2 %collective-permute-start.9 = (bf16[4,80,128]{2,1,0:T(8,128)(2,1)S(1)}, bf16[4,80,128]{2,1,0:T(8,128)(2,1)S(1)}, u32[]{:S(2)}, u32[]{:S(2)}) collective-permute-start(bf16[4,80,128]{2,1,0:T(8,128)(2,1)S(1)} %get-tuple-element.18), channel_id=1, source_target_pairs={{0,48},{8,56},{16,32},{24,40},{32,16},{40,24},{48,0},{56,8},{64,11... | collective-permute-start | bytes 245768 | tf_op jit(solution)/shard_map/ppermute | solution.py:31
  26.2 1.6 %read.4 = bf16[4,80,128]{2,1,0:T(8,128)(2,1)S(1)} custom-call(bf16[4,80,128]{2,1,0:T(8,128)(2,1)S(1)} %collective-permute-done.5.refs_0_, bf16[2048,128]{1,0:T(8,128)(2,1)S(1)} %get-tuple-element.16.refs_1_.refs_2_, bf16[128,2048]{1,0:T(8,128)(2,1)S(1)} %get-tuple-element.17.refs_2_.refs_3_, bf16[2048,128]{1,0:T(8,128)(2,1)S(1)} %collective-permute-done.3.refs_3_.refs_4_, ...), custom_call_target="tpu_custom_call" | custom-call | flops 671088640 | bytes 4194304 | tf_op jit(solution)/shard_map/read/pallas_call | solution.py:134
  27.8 2.4 %collective-permute-start.6 = (bf16[4,80,128]{2,1,0:T(8,128)(2,1)S(1)}, bf16[4,80,128]{2,1,0:T(8,128)(2,1)S(1)}, u32[]{:S(2)}, u32[]{:S(2)}) collective-permute-start(bf16[4,80,128]{2,1,0:T(8,128)(2,1)S(1)} %read.4), channel_id=1, source_target_pairs={{0,40},{8,32},{16,56},{24,48},{32,8},{40,0},{48,24},{56,16},{64,10... | collective-permute-start | bytes 245768 | tf_op jit(solution)/shard_map/ppermute | solution.py:31
  30.2 1.6 %read.3.refs_0_ = bf16[4,80,128]{2,1,0:T(8,128)(2,1)S(1)} custom-call(bf16[4,80,128]{2,1,0:T(8,128)(2,1)S(1)} %join.1.refs_0_, bf16[2048,128]{1,0:T(8,128)(2,1)S(1)} %get-tuple-element.16.refs_1_.refs_2_, bf16[128,2048]{1,0:T(8,128)(2,1)S(1)} %get-tuple-element.17.refs_2_.refs_3_, bf16[2048,128]{1,0:T(8,128)(2,1)S(1)} %collective-permute-done.3.refs_3_.refs_4_, ...), custom_call_target="tpu_custom_call" | custom-call | flops 671088640 | bytes 4194304 | tf_op jit(solution)/shard_map/read/pallas_call | solution.py:134
  31.8 2.0 %collective-permute-done.6.refs_1_ = bf16[4,80,128]{2,1,0:T(8,128)(2,1)S(1)} collective-permute-done((bf16[4,80,128]{2,1,0:T(8,128)(2,1)S(1)}, bf16[4,80,128]{2,1,0:T(8,128)(2,1)S(1)}, u32[]{:S(2)}, u32[]{:S(2)}) %collective-permute-start.6) | collective-permute-done | bytes 81952 | tf_op jit(solution)/shard_map/ppermute | solution.py:31
  33.8 5.1 %collective-permute-start.11 = (bf16[80,128]{1,0:T(8,128)(2,1)S(1)}, bf16[80,128]{1,0:T(8,128)(2,1)S(1)}, u32[]{:S(2)}, u32[]{:S(2)}) collective-permute-start(bf16[80,128]{1,0:T(8,128)(2,1)S(1)} %get-tuple-element.21), channel_id=1, source_target_pairs={{0,136},{8,128},{16,152},{24,144},{32,168},{40,160},{48,184},{56,1... | collective-permute-start | bytes 61448 | tf_op jit(solution)/shard_map/ppermute | solution.py:31
  38.9 1.5 %collective-permute-start.13 = (bf16[80,128]{1,0:T(8,128)(2,1)S(1)}, bf16[80,128]{1,0:T(8,128)(2,1)S(1)}, u32[]{:S(2)}, u32[]{:S(2)}) collective-permute-start(bf16[80,128]{1,0:T(8,128)(2,1)S(1)} %get-tuple-element.23), channel_id=1, source_target_pairs={{0,64},{8,72},{16,80},{24,88},{32,96},{40,104},{48,112},{56,120},{... | collective-permute-start | bytes 61448 | tf_op jit(solution)/shard_map/ppermute | solution.py:31
  40.4 1.7 %fetch.2.refs_5_ = bf16[256,5120]{1,0:T(8,128)(2,1)S(1)} custom-call(bf16[640,5120]{1,0:T(8,128)(2,1)} %w_hbm.3), custom_call_target="tpu_custom_call" | custom-call | bytes 4194304 | tf_op jit(solution)/shard_map/fetch/pallas_call | solution.py:154
  42.1 2.1 %fetch.3.refs_6_ = bf16[384,5120]{1,0:T(8,128)(2,1)S(1)} custom-call(bf16[640,5120]{1,0:T(8,128)(2,1)} %w_hbm.3), custom_call_target="tpu_custom_call" | custom-call | bytes 4194304 | tf_op jit(solution)/shard_map/fetch/pallas_call | solution.py:154
  44.3 1.1 %project.1 = bf16[8,16,640]{2,1,0:T(8,128)(2,1)S(1)} custom-call(bf16[80,128]{1,0:T(8,128)(2,1)S(1)} %get-tuple-element.20.refs_0_, bf16[80,128]{1,0:T(8,128)(2,1)S(1)} %collective-permute-done.11.refs_1_, bf16[80,128]{1,0:T(8,128)(2,1)S(1)} %collective-permute-done.12.refs_2_, bf16[80,128]{1,0:T(8,128)(2,1)S(1)} %collective-permute-done.13.refs_3_, ...), custom_call_target="tpu_custom_call" | custom-call | tf_op jit(solution)/shard_map/project/pallas_call | solution.py:219
  45.3 12.6 %all_to_all.5 = bf16[8,16,640]{2,1,0:T(8,128)(2,1)S(1)} all-to-all(bf16[8,16,640]{2,1,0:T(8,128)(2,1)S(1)} %project.1), channel_id=1, replica_groups=mesh['seq'=32,'head'=8] {'head'}, dimensions={0} | all-to-all | bytes 327680 | tf_op jit(solution)/shard_map/all_to_all | solution.py:262
  57.9 0.6 %reduce_sum.12 = bf16[16,640]{1,0:T(8,128)(2,1)} reduce(bf16[8,16,640]{2,1,0:T(8,128)(2,1)S(1)} %all_to_all.5, bf16[]{:T(256)} %constant.2.clone.1), dimensions={0}, to_apply=%region_0.0 | reduce | flops 71680 | bytes 184322 | tf_op jit(solution)/shard_map/reduce_sum | solution.py:263
  (15 shorter events, 0.1 us)
Async XLA Ops:
  0.0 21.6 %collective-permute-start.3 = (bf16[2048,128]{1,0:T(8,128)(2,1)}, bf16[2048,128]{1,0:T(8,128)(2,1)S(1)}, u32[]{:S(2)}, u32[]{:S(2)}) collective-permute-start(bf16[2048,128]{1,0:T(8,128)(2,1)} %bitcast.6), channel_id=1, source_target_pairs={{0,8},{8,0},{16,24},{24,16},{32,40},{40,32},{48,56},{56,48},{64,72... | collective-permute-start | bytes 1572872 | tf_op jit(solution)/shard_map/ppermute | solution.py:240
  1.3 20.3 %collective-permute-start.4 = (bf16[128,2048]{1,0:T(8,128)(2,1)S(1)}, bf16[128,2048]{1,0:T(8,128)(2,1)S(1)}, u32[]{:S(2)}, u32[]{:S(2)}) collective-permute-start(bf16[128,2048]{1,0:T(8,128)(2,1)S(1)} %get-tuple-element.17.refs_2_.refs_3_), channel_id=1, source_target_pairs={{0,8},{8,0},{16,24},{24,16},{32,40},{40,32},{48,56},{56,48},{64,72... | collective-permute-start | bytes 1572872 | tf_op jit(solution)/shard_map/ppermute | solution.py:242
  1.9 7.6 %collective-permute-start.2 = (bf16[80,128]{1,0:T(8,128)(2,1)}, bf16[80,128]{1,0:T(8,128)(2,1)S(1)}, u32[]{:S(2)}, u32[]{:S(2)}) collective-permute-start(bf16[80,128]{1,0:T(8,128)(2,1)} %bitcast.9), channel_id=1, source_target_pairs={{0,200},{8,192},{16,216},{24,208},{32,232},{40,224},{48,248},{56,2... | collective-permute-start | bytes 61448 | tf_op jit(solution)/shard_map/ppermute | solution.py:31
  7.0 7.3 %collective-permute-start.1 = (bf16[80,128]{1,0:T(8,128)(2,1)}, bf16[80,128]{1,0:T(8,128)(2,1)S(1)}, u32[]{:S(2)}, u32[]{:S(2)}) collective-permute-start(bf16[80,128]{1,0:T(8,128)(2,1)} %bitcast.10), channel_id=1, source_target_pairs={{0,136},{8,128},{16,152},{24,144},{32,168},{40,160},{48,184},{56,1... | collective-permute-start | bytes 61448 | tf_op jit(solution)/shard_map/ppermute | solution.py:31
  8.4 5.9 %collective-permute-start = (bf16[80,128]{1,0:T(8,128)(2,1)}, bf16[80,128]{1,0:T(8,128)(2,1)S(1)}, u32[]{:S(2)}, u32[]{:S(2)}) collective-permute-start(bf16[80,128]{1,0:T(8,128)(2,1)} %bitcast.11), channel_id=1, source_target_pairs={{0,64},{8,72},{16,80},{24,88},{32,96},{40,104},{48,112},{56,120},{... | collective-permute-start | bytes 61448 | tf_op jit(solution)/shard_map/ppermute | solution.py:31
  14.3 4.2 %collective-permute-start.8 = (bf16[4,80,128]{2,1,0:T(8,128)(2,1)S(1)}, bf16[4,80,128]{2,1,0:T(8,128)(2,1)S(1)}, u32[]{:S(2)}, u32[]{:S(2)}) collective-permute-start(bf16[4,80,128]{2,1,0:T(8,128)(2,1)S(1)} %join.1.refs_0_), channel_id=1, source_target_pairs={{0,24},{8,16},{16,8},{24,0},{32,56},{40,48},{48,40},{56,32},{64,88... | collective-permute-start | bytes 245768 | tf_op jit(solution)/shard_map/ppermute | solution.py:31
  15.9 5.7 %collective-permute-start.7 = (bf16[4,80,128]{2,1,0:T(8,128)(2,1)S(1)}, bf16[4,80,128]{2,1,0:T(8,128)(2,1)S(1)}, u32[]{:S(2)}, u32[]{:S(2)}) collective-permute-start(bf16[4,80,128]{2,1,0:T(8,128)(2,1)S(1)} %join.1.refs_0_), channel_id=1, source_target_pairs={{0,48},{8,56},{16,32},{24,40},{32,16},{40,24},{48,0},{56,8},{64,11... | collective-permute-start | bytes 245768 | tf_op jit(solution)/shard_map/ppermute | solution.py:31
  18.0 8.2 %collective-permute-start.5 = (bf16[4,80,128]{2,1,0:T(8,128)(2,1)S(1)}, bf16[4,80,128]{2,1,0:T(8,128)(2,1)S(1)}, u32[]{:S(2)}, u32[]{:S(2)}) collective-permute-start(bf16[4,80,128]{2,1,0:T(8,128)(2,1)S(1)} %join.1.refs_0_), channel_id=1, source_target_pairs={{0,40},{8,32},{16,56},{24,48},{32,8},{40,0},{48,24},{56,16},{64,10... | collective-permute-start | bytes 245768 | tf_op jit(solution)/shard_map/ppermute | solution.py:31
  24.0 7.7 %collective-permute-start.9 = (bf16[4,80,128]{2,1,0:T(8,128)(2,1)S(1)}, bf16[4,80,128]{2,1,0:T(8,128)(2,1)S(1)}, u32[]{:S(2)}, u32[]{:S(2)}) collective-permute-start(bf16[4,80,128]{2,1,0:T(8,128)(2,1)S(1)} %get-tuple-element.18), channel_id=1, source_target_pairs={{0,48},{8,56},{16,32},{24,40},{32,16},{40,24},{48,0},{56,8},{64,11... | collective-permute-start | bytes 245768 | tf_op jit(solution)/shard_map/ppermute | solution.py:31
  26.2 5.6 %collective-permute-start.10 = (bf16[4,80,128]{2,1,0:T(8,128)(2,1)S(1)}, bf16[4,80,128]{2,1,0:T(8,128)(2,1)S(1)}, u32[]{:S(2)}, u32[]{:S(2)}) collective-permute-start(bf16[4,80,128]{2,1,0:T(8,128)(2,1)S(1)} %get-tuple-element.19), channel_id=1, source_target_pairs={{0,24},{8,16},{16,8},{24,0},{32,56},{40,48},{48,40},{56,32},{64,88... | collective-permute-start | bytes 245768 | tf_op jit(solution)/shard_map/ppermute | solution.py:31
  27.8 6.0 %collective-permute-start.6 = (bf16[4,80,128]{2,1,0:T(8,128)(2,1)S(1)}, bf16[4,80,128]{2,1,0:T(8,128)(2,1)S(1)}, u32[]{:S(2)}, u32[]{:S(2)}) collective-permute-start(bf16[4,80,128]{2,1,0:T(8,128)(2,1)S(1)} %read.4), channel_id=1, source_target_pairs={{0,40},{8,32},{16,56},{24,48},{32,8},{40,0},{48,24},{56,16},{64,10... | collective-permute-start | bytes 245768 | tf_op jit(solution)/shard_map/ppermute | solution.py:31
  33.8 10.4 %collective-permute-start.11 = (bf16[80,128]{1,0:T(8,128)(2,1)S(1)}, bf16[80,128]{1,0:T(8,128)(2,1)S(1)}, u32[]{:S(2)}, u32[]{:S(2)}) collective-permute-start(bf16[80,128]{1,0:T(8,128)(2,1)S(1)} %get-tuple-element.21), channel_id=1, source_target_pairs={{0,136},{8,128},{16,152},{24,144},{32,168},{40,160},{48,184},{56,1... | collective-permute-start | bytes 61448 | tf_op jit(solution)/shard_map/ppermute | solution.py:31
  38.9 5.4 %collective-permute-start.12 = (bf16[80,128]{1,0:T(8,128)(2,1)S(1)}, bf16[80,128]{1,0:T(8,128)(2,1)S(1)}, u32[]{:S(2)}, u32[]{:S(2)}) collective-permute-start(bf16[80,128]{1,0:T(8,128)(2,1)S(1)} %get-tuple-element.22), channel_id=1, source_target_pairs={{0,200},{8,192},{16,216},{24,208},{32,232},{40,224},{48,248},{56,2... | collective-permute-start | bytes 61448 | tf_op jit(solution)/shard_map/ppermute | solution.py:31
  38.9 5.4 %collective-permute-start.13 = (bf16[80,128]{1,0:T(8,128)(2,1)S(1)}, bf16[80,128]{1,0:T(8,128)(2,1)S(1)}, u32[]{:S(2)}, u32[]{:S(2)}) collective-permute-start(bf16[80,128]{1,0:T(8,128)(2,1)S(1)} %get-tuple-element.23), channel_id=1, source_target_pairs={{0,64},{8,72},{16,80},{24,88},{32,96},{40,104},{48,112},{56,120},{... | collective-permute-start | bytes 61448 | tf_op jit(solution)/shard_map/ppermute | solution.py:31
